TPU v7x, 128 devices: a whole 4x4x4 slice. The times are simulated.
128 devices in a mesh: dp: 8 (over y, core), expert: 16 (over x, z).
Axes of the slice: x: 4, y: 4, z: 4, core: 2. Of those that a mesh axis runs over, the one named last changes fastest.
Arguments:
- tokens: bfloat16 [16384, 4096], P(('dp', 'expert')), may hold values from -6 to 6
- expert_ids: int32 [16384, 2], P(('dp', 'expert')), may hold values from 0 to 63, all different within a row; in each aligned block of 128 rows (0 to 127, 128 to 255, ...) at most 6 rows name the same one
- gate_num: int32 [16384, 2], P(('dp', 'expert')), may hold values from 1 to 255
- out_grad: bfloat16 [16384, 4096], P(('dp', 'expert')), may hold values from -6 to 6
- gate_weight: bfloat16 [128, 4096, 384], P(('dp', 'expert')), may hold values from -0.09375 to 0.09375
- up_weight: bfloat16 [128, 4096, 384], P(('dp', 'expert')), may hold values from -0.09375 to 0.09375
- down_weight: bfloat16 [128, 384, 4096], P(('dp', 'expert')), may hold values from -0.21875 to 0.21875
Outputs:
- moe_out: bfloat16 [16384, 4096], P(('dp', 'expert'))
- token_grad: bfloat16 [16384, 4096], P(('dp', 'expert'))
- gate_grad: bfloat16 [128, 4096, 384], P(('dp', 'expert'))
- up_grad: bfloat16 [128, 4096, 384], P(('dp', 'expert'))
- down_grad: bfloat16 [128, 384, 4096], P(('dp', 'expert'))
Inputs may be any that keep to these rules, and one draw needn't show every extreme that they name: `expert_ids`: each token names 2 different experts; among the 128 tokens of one device no expert is named by more than 6 routes, a bound that some block reaches. A route's gate weight is gate_num / 256.
All inputs are finite; a program needn't handle non-finite values.
Results may differ from a plain program's by a relative error of at most 0.0065.
Values may be sent and summed in bfloat16 or wider, within the bound.
A program may use at most 256 MiB of HBM per device.

v0:
```python
import jax
import jax.numpy as jnp
from jax import lax
from jax.sharding import PartitionSpec as P

DEN = 256


def route_slots(expert_ids, gate_num, expert_count, capacity):
    tok_rows, route_count = expert_ids.shape
    flat_ids = expert_ids.reshape(-1)
    onehot = (flat_ids[:, None] == jnp.arange(expert_count, dtype=jnp.int32)[None, :]).astype(
        jnp.int32
    )
    before = jnp.cumsum(onehot, axis=0) - onehot
    route_rank = jnp.sum(before * onehot, axis=1)
    slot_of_route = flat_ids * capacity + route_rank
    matched = (
        slot_of_route[None, :] == jnp.arange(expert_count * capacity, dtype=jnp.int32)[:, None]
    )
    gate_values = gate_num.reshape(-1).astype(jnp.float32) / DEN
    placer = jnp.sum(matched.reshape(-1, tok_rows, route_count).astype(jnp.int32), axis=2).astype(
        jnp.bfloat16
    )
    weigher = jnp.sum(
        jnp.where(matched, gate_values[None, :], 0.0).reshape(-1, tok_rows, route_count), axis=2
    )
    return (placer, weigher.astype(jnp.bfloat16))


def return_home(partial_value, expert_count, capacity):
    width = partial_value.shape[-1]
    part_rows = partial_value.reshape(-1, capacity, width)
    received = lax.all_to_all(part_rows, ("dp", "expert"), split_axis=0, concat_axis=0, tiled=True)
    halves = received.reshape(2, expert_count, capacity, width)
    summed = (halves[0] + halves[1]).astype(jnp.bfloat16)
    return summed.reshape(expert_count * capacity, width)


def on_device(tokens, expert_ids, gate_num, out_grad, gate_weight, up_weight, down_weight):
    dp_count = lax.axis_size("dp")
    group_count = lax.axis_size("expert")
    device_count = dp_count * group_count
    expert_count = device_count // 2
    tok_rows, route_count = expert_ids.shape
    width = tokens.shape[1]
    capacity = 2 * ((3 * tok_rows * route_count + 4 * expert_count - 1) // (4 * expert_count))
    placer, weigher = route_slots(expert_ids, gate_num, expert_count, capacity)
    x_slots = jnp.dot(placer, tokens, preferred_element_type=jnp.float32).astype(jnp.bfloat16)
    g_slots = jnp.dot(weigher, out_grad, preferred_element_type=jnp.float32).astype(jnp.bfloat16)
    x_slots = x_slots.reshape(expert_count, capacity, width)
    g_slots = g_slots.reshape(expert_count, capacity, width)
    send_rows = jnp.concatenate([x_slots, x_slots], axis=0)
    send_grads = jnp.concatenate([g_slots, g_slots], axis=0)
    rows_in, grads_in = (
        lax.all_to_all(send_rows, ("dp", "expert"), split_axis=0, concat_axis=0, tiled=True),
        lax.all_to_all(send_grads, ("dp", "expert"), split_axis=0, concat_axis=0, tiled=True),
    )
    rows_in = rows_in.reshape(-1, width)
    grads_in = grads_in.reshape(-1, width)
    gate_block = gate_weight[0]
    up_block = up_weight[0]
    down_block = down_weight[0]
    gate_act = jnp.dot(rows_in, gate_block, preferred_element_type=jnp.float32)
    up_act = jnp.dot(rows_in, up_block, preferred_element_type=jnp.float32)
    sigmoid_gate = jax.nn.sigmoid(gate_act)
    silu_gate = gate_act * sigmoid_gate
    hidden = (silu_gate * up_act).astype(jnp.bfloat16)
    partial_out = jnp.dot(hidden, down_block, preferred_element_type=jnp.float32)
    expert_out = return_home(partial_out, expert_count, capacity)
    contract_last = (((1,), (1,)), ((), ()))
    contract_first = (((0,), (0,)), ((), ()))
    moe_out = lax.dot_general(
        weigher, expert_out, contract_first, preferred_element_type=jnp.float32
    )
    hidden_grad = lax.dot_general(
        grads_in, down_block, contract_last, preferred_element_type=jnp.float32
    )
    down_grad = lax.dot_general(
        hidden, grads_in, contract_first, preferred_element_type=jnp.float32
    )
    up_grad_act = (hidden_grad * silu_gate).astype(jnp.bfloat16)
    gate_grad_act = (
        hidden_grad * up_act * sigmoid_gate * (1.0 + gate_act * (1.0 - sigmoid_gate))
    ).astype(jnp.bfloat16)
    gate_grad = lax.dot_general(
        rows_in, gate_grad_act, contract_first, preferred_element_type=jnp.float32
    )
    up_grad = lax.dot_general(
        rows_in, up_grad_act, contract_first, preferred_element_type=jnp.float32
    )
    row_part = lax.dot_general(
        gate_grad_act, gate_block, contract_last, preferred_element_type=jnp.float32
    )
    row_part = row_part + lax.dot_general(
        up_grad_act, up_block, contract_last, preferred_element_type=jnp.float32
    )
    row_grad = return_home(row_part, expert_count, capacity)
    token_grad = lax.dot_general(
        placer, row_grad, contract_first, preferred_element_type=jnp.float32
    )
    return (
        moe_out.astype(jnp.bfloat16),
        token_grad.astype(jnp.bfloat16),
        gate_grad.astype(jnp.bfloat16)[None],
        up_grad.astype(jnp.bfloat16)[None],
        down_grad.astype(jnp.bfloat16)[None],
    )


def solution(mesh):
    in_specs = (
        P(("dp", "expert"), None),
        P(("dp", "expert"), None),
        P(("dp", "expert"), None),
        P(("dp", "expert"), None),
        P(("dp", "expert"), None, None),
        P(("dp", "expert"), None, None),
        P(("dp", "expert"), None, None),
    )
    out_specs = (
        P(("dp", "expert"), None),
        P(("dp", "expert"), None),
        P(("dp", "expert"), None, None),
        P(("dp", "expert"), None, None),
        P(("dp", "expert"), None, None),
    )
    return jax.shard_map(
        on_device, mesh=mesh, in_specs=in_specs, out_specs=out_specs, check_vma=False
    )
```

profile of v0, /device:TPU:1, one launch (start us, length us, event | category | flops | bytes accessed | tf_op | source)
XLA Modules:
  0.0 800.3 jit_solution(16392336765472285899)
XLA Ops:
  3.8 3.9 convolution_convert_fusion.4
  7.7 5.6 reshape.103
  13.3 8.4 %pad_maximum_fusion = bf16[128,6,4096]{2,1,0:T(8,128)(2,1)} fusion(bf16[64,6,4096]{2,1,0:T(8,128)(2,1)} %reshape.103), kind=kLoop, calls=%fused_computation.4 | loop fusion | flops 3145728 | bytes 9437184 | tf_op jit(solution)/shard_map/concatenate | solution.py:53
  21.7 12.0 %all-to-all-start = ((bf16[128,6,4096]{2,1,0:T(8,128)(2,1)}), bf16[128,6,4096]{2,1,0:T(8,128)(2,1)}, u32[]{:S(2)}, u32[]{:S(2)}) async-start(bf16[128,6,4096]{2,1,0:T(8,128)(2,1)} %pad_maximum_fusion), calls=%async_computation | async-start | bytes 16777216 | tf_op jit(solution)/shard_map/all_to_all | solution.py:56
  33.7 3.9 convolution_convert_fusion.3
  37.6 5.6 reshape.105
  43.2 8.4 %pad_maximum_fusion.1 = bf16[128,6,4096]{2,1,0:T(8,128)(2,1)} fusion(bf16[64,6,4096]{2,1,0:T(8,128)(2,1)} %reshape.105), kind=kLoop, calls=%fused_computation.5 | loop fusion | flops 3145728 | bytes 9437184 | tf_op jit(solution)/shard_map/concatenate | solution.py:54
  51.6 83.3 %all-to-all-done = bf16[128,6,4096]{2,1,0:T(8,128)(2,1)} async-done(((bf16[128,6,4096]{2,1,0:T(8,128)(2,1)}), bf16[128,6,4096]{2,1,0:T(8,128)(2,1)}, u32[]{:S(2)}, u32[]{:S(2)}) %all-to-all-start) | async-done | bytes 6291488 | tf_op jit(solution)/shard_map/all_to_all | solution.py:56
  134.9 10.6 %all-to-all-start.2 = ((bf16[128,6,4096]{2,1,0:T(8,128)(2,1)}), bf16[128,6,4096]{2,1,0:T(8,128)(2,1)}, u32[]{:S(2)}, u32[]{:S(2)}) async-start(bf16[128,6,4096]{2,1,0:T(8,128)(2,1)} %pad_maximum_fusion.1), calls=%async_computation.2 | async-start | bytes 16777216 | tf_op jit(solution)/shard_map/all_to_all | solution.py:57
  145.5 10.2 %reshape.104 = bf16[768,4096]{1,0:T(8,128)(2,1)} reshape(bf16[128,6,4096]{2,1,0:T(8,128)(2,1)} %all-to-all-done) | data formatting | bytes 12582912 | tf_op jit(solution)/shard_map/reshape | solution.py:59
  155.7 8.3 %fusion.10 = f32[768,384]{1,0:T(8,128)} fusion(bf16[768,4096]{1,0:T(8,128)(2,1)} %reshape.104, bf16[1,4096,384]{2,1,0:T(8,128)(2,1)} %param.12), kind=kOutput, calls=%fused_computation.22 | convolution fusion | flops 2415919104 | bytes 10616832 | tf_op jit(solution)/shard_map/dot_general | solution.py:65
  163.9 4.4 fusion.14
  168.4 77.2 %all-to-all-done.2 = bf16[128,6,4096]{2,1,0:T(8,128)(2,1)} async-done(((bf16[128,6,4096]{2,1,0:T(8,128)(2,1)}), bf16[128,6,4096]{2,1,0:T(8,128)(2,1)}, u32[]{:S(2)}, u32[]{:S(2)}) %all-to-all-start.2) | async-done | bytes 6291488 | tf_op jit(solution)/shard_map/all_to_all | solution.py:57
  245.6 10.2 %reshape.106 = bf16[768,4096]{1,0:T(8,128)(2,1)} reshape(bf16[128,6,4096]{2,1,0:T(8,128)(2,1)} %all-to-all-done.2) | data formatting | bytes 12582912 | tf_op jit(solution)/shard_map/reshape | solution.py:60
  255.8 8.4 %multiply_convert_fusion = (bf16[768,384]{1,0:T(8,128)(2,1)}, bf16[768,384]{1,0:T(8,128)(2,1)}, bf16[768,384]{1,0:T(8,128)(2,1)}) fusion(f32[768,384]{1,0:T(8,128)} %fusion.14, f32[768,384]{1,0:T(8,128)} %fusion.10, bf16[768,4096]{1,0:T(8,128)(2,1)} %reshape.106, bf16[1,384,4096]{2,1,0:T(8,128)(2,1)S(1)} %copy-done), kind=kOutput, calls=%fused_computation.28 | convolution fusion | flops 2420342784 | bytes 13565952 | tf_op jit(solution)/shard_map/dot_general | solution.py:76
  266.3 7.5 fusion.5
  273.8 17.8 %copy.44 = f32[128,6,4096]{2,1,0:T(8,128)} copy(f32[128,6,4096]{2,0,1:T(8,128)} %fusion.5) | data formatting | bytes 25165824 | tf_op jit(solution)/shard_map/dot_general | solution.py:69
  291.7 10.8 %all-to-all-start.1 = ((f32[128,6,4096]{2,1,0:T(8,128)}), f32[128,6,4096]{2,1,0:T(8,128)}, u32[]{:S(2)}, u32[]{:S(2)}) async-start(f32[128,6,4096]{2,1,0:T(8,128)} %copy.44), calls=%async_computation.1 | async-start | bytes 33554432 | tf_op jit(solution)/shard_map/all_to_all | solution.py:34
  302.4 5.7 fusion.12
  308.1 6.4 convolution_add_fusion
  314.5 13.9 %reshape.107 = f32[128,6,4096]{2,1,0:T(8,128)} reshape(f32[768,4096]{1,0:T(8,128)} %convolution_add_fusion) | data formatting | bytes 25165824 | tf_op jit(solution)/shard_map/reshape | solution.py:33
  328.4 211.0 %all-to-all-done.1 = f32[128,6,4096]{2,1,0:T(8,128)} async-done(((f32[128,6,4096]{2,1,0:T(8,128)}), f32[128,6,4096]{2,1,0:T(8,128)}, u32[]{:S(2)}, u32[]{:S(2)}) %all-to-all-start.1) | async-done | bytes 12582944 | tf_op jit(solution)/shard_map/all_to_all | solution.py:34
  539.4 9.2 %all-to-all-start.3 = ((f32[128,6,4096]{2,1,0:T(8,128)}), f32[128,6,4096]{2,1,0:T(8,128)}, u32[]{:S(2)}, u32[]{:S(2)}) async-start(f32[128,6,4096]{2,1,0:T(8,128)} %reshape.107), calls=%async_computation.3 | async-start | bytes 33554432 | tf_op jit(solution)/shard_map/all_to_all | solution.py:34
  548.6 7.3 fusion.4
  555.9 8.1 %fusion.3 = bf16[1,4096,384]{2,1,0:T(8,128)(2,1)} fusion(bf16[768,4096]{1,0:T(8,128)(2,1)} %reshape.104, bf16[768,384]{1,0:T(8,128)(2,1)S(1)} %copy-done.7), kind=kOutput, calls=%fused_computation.13 | convolution fusion | flops 2417491968 | bytes 10027008 | tf_op jit(solution)/shard_map/dot_general | solution.py:89
  564.0 4.8 fusion.2
  568.8 8.5 %fusion.1 = bf16[64,6,4096]{2,1,0:T(8,128)(2,1)} fusion(f32[128,6,4096]{2,1,0:T(8,128)} %all-to-all-done.1), kind=kLoop, calls=%fused_computation.3 | loop fusion | flops 3145728 | bytes 15728640 | tf_op jit(solution)/shard_map/convert_element_type | solution.py:36
  577.3 4.2 convert_element_type.76
  583.2 198.9 %all-to-all-done.3 = f32[128,6,4096]{2,1,0:T(8,128)} async-done(((f32[128,6,4096]{2,1,0:T(8,128)}), f32[128,6,4096]{2,1,0:T(8,128)}, u32[]{:S(2)}, u32[]{:S(2)}) %all-to-all-start.3) | async-done | bytes 12582944 | tf_op jit(solution)/shard_map/all_to_all | solution.py:34
  782.1 8.6 %fusion = bf16[64,6,4096]{2,1,0:T(8,128)(2,1)} fusion(f32[128,6,4096]{2,1,0:T(8,128)} %all-to-all-done.3), kind=kLoop, calls=%fused_computation.1 | loop fusion | flops 3145728 | bytes 15728640 | tf_op jit(solution)/shard_map/convert_element_type | solution.py:36
  790.7 5.7 convert_element_type.82
  796.4 3.6 convolution_convert_fusion.5
  (42 shorter events, 7.0 us)
Async XLA Ops:
  0.6 255.2 %copy-start = (bf16[1,384,4096]{2,1,0:T(8,128)(2,1)S(1)}, bf16[1,384,4096]{2,1,0:T(8,128)(2,1)}, u32[]{:S(2)}) copy-start(bf16[1,384,4096]{2,1,0:T(8,128)(2,1)} %param.13) | copy-start | bytes 9437188
  21.7 12.0 %copy-start.9 = (s32[128,2]{0,1:T(2,128)S(1)}, s32[128,2]{0,1:T(2,128)}, u32[]{:S(2)}) copy-start(s32[128,2]{0,1:T(2,128)} %param.9) | copy-start | bytes 3076
  21.7 113.2 %all-to-all-start = ((bf16[128,6,4096]{2,1,0:T(8,128)(2,1)}), bf16[128,6,4096]{2,1,0:T(8,128)(2,1)}, u32[]{:S(2)}, u32[]{:S(2)}) async-start(bf16[128,6,4096]{2,1,0:T(8,128)(2,1)} %pad_maximum_fusion), calls=%async_computation | async-start | bytes 16777216 | tf_op jit(solution)/shard_map/all_to_all | solution.py:56
  134.9 110.7 %all-to-all-start.2 = ((bf16[128,6,4096]{2,1,0:T(8,128)(2,1)}), bf16[128,6,4096]{2,1,0:T(8,128)(2,1)}, u32[]{:S(2)}, u32[]{:S(2)}) async-start(bf16[128,6,4096]{2,1,0:T(8,128)(2,1)} %pad_maximum_fusion.1), calls=%async_computation.2 | async-start | bytes 16777216 | tf_op jit(solution)/shard_map/all_to_all | solution.py:57
  155.7 8.3 %copy-start.2 = (bf16[768,4096]{1,0:T(8,128)(2,1)S(1)}, bf16[768,4096]{1,0:T(8,128)(2,1)}, u32[]{:S(2)}) copy-start(bf16[768,4096]{1,0:T(8,128)(2,1)} %reshape.104) | copy-start | bytes 18874372
  155.7 8.3 %copy-start.5 = (bf16[1,4096,384]{2,1,0:T(8,128)(2,1)S(1)}, bf16[1,4096,384]{2,1,0:T(8,128)(2,1)}, u32[]{:S(2)}) copy-start(bf16[1,4096,384]{2,1,0:T(8,128)(2,1)} %param.11) | copy-start | bytes 9437188
  291.7 247.7 %all-to-all-start.1 = ((f32[128,6,4096]{2,1,0:T(8,128)}), f32[128,6,4096]{2,1,0:T(8,128)}, u32[]{:S(2)}, u32[]{:S(2)}) async-start(f32[128,6,4096]{2,1,0:T(8,128)} %copy.44), calls=%async_computation.1 | async-start | bytes 33554432 | tf_op jit(solution)/shard_map/all_to_all | solution.py:34
  302.4 5.7 copy-start.4
  302.4 5.7 copy-start.6
  328.4 220.2 %copy-start.3 = (bf16[768,384]{1,0:T(8,128)(2,1)S(1)}, bf16[768,384]{1,0:T(8,128)(2,1)}, u32[]{:S(2)}) copy-start(bf16[768,384]{1,0:T(8,128)(2,1)} %get-tuple-element.7) | copy-start | bytes 1769476
  539.4 242.7 %all-to-all-start.3 = ((f32[128,6,4096]{2,1,0:T(8,128)}), f32[128,6,4096]{2,1,0:T(8,128)}, u32[]{:S(2)}, u32[]{:S(2)}) async-start(f32[128,6,4096]{2,1,0:T(8,128)} %reshape.107), calls=%async_computation.3 | async-start | bytes 33554432 | tf_op jit(solution)/shard_map/all_to_all | solution.py:34
  548.6 7.3 copy-start.7
  548.6 15.3 %slice-start = ((s8[6291456]{0:T(1024)(128)(4,1)}), s8[4194304]{0:T(1024)(128)(4,1)S(1)}, s32[]{:S(2)}) async-start(s8[6291456]{0:T(1024)(128)(4,1)} %bitcast.60), calls=%async_computation.4 | async-start | bytes 8388608
  555.9 8.1 %slice-start.1 = ((s8[6291456]{0:T(1024)(128)(4,1)}), s8[2097152]{0:T(1024)(128)(4,1)S(1)}, s32[]{:S(2)}) async-start(s8[6291456]{0:T(1024)(128)(4,1)} %bitcast.60), calls=%async_computation.5 | async-start | bytes 4194304
  555.9 8.1 %copy-start.8 = (bf16[768,384]{1,0:T(8,128)(2,1)S(1)}, bf16[768,384]{1,0:T(8,128)(2,1)}, u32[]{:S(2)}) copy-start(bf16[768,384]{1,0:T(8,128)(2,1)} %get-tuple-element.6) | copy-start | bytes 1769476
  782.1 17.9 %copy-start.1 = (bf16[1,384,4096]{2,1,0:T(8,128)(2,1)S(1)}, bf16[1,384,4096]{2,1,0:T(8,128)(2,1)}, u32[]{:S(2)}) copy-start(bf16[1,384,4096]{2,1,0:T(8,128)(2,1)} %param.13) | copy-start | bytes 9437188
where the time goes:
time: 816 us; the launch traced here: 800 us
  waiting for transfers between devices  570 us (70%)
  local copies, waits for them, and re-layouts  77.1 us (9%)
  matrix products  73.9 us (9%)
  starting transfers between devices  42.5 us (5%)
  other arithmetic  35.4 us (4%)
    all_to_all x2, waiting for transfers between devices, return_home(): lax.all_to_all(part_rows, ('dp', 'expert'), split_axis=0, concat_axis=0,...  410 us
    all_to_all x1, waiting for transfers between devices, on_device(): lax.all_to_all(send_rows, ('dp', 'expert'), split_axis=0, concat_axis=0,...  83.3 us
    all_to_all x1, waiting for transfers between devices, on_device(): lax.all_to_all(send_grads, ('dp', 'expert'), split_axis=0, concat_axis=0,...  77.2 us
    all_to_all x2, starting transfers between devices, return_home(): lax.all_to_all(part_rows, ('dp', 'expert'), split_axis=0, concat_axis=0,...  19.9 us
    dot_general x2, local copies, waits for them, and re-layouts, on_device(): jnp.dot(hidden, down_block, preferred_element_type=jnp.float32)  19.9 us
    convert_element_type x2, other arithmetic, return_home(): summed = (halves[0] + halves[1]).astype(jnp.bfloat16)  17.1 us
  transfers between devices with their start and end apart: 4, of which 4 were waited for; matrix products, arithmetic and copies ran while one was open for 13% of the time, Pallas kernels for 0%

commit v1 on v0

v1 whole, which is shorter than its diff:
```python
import jax
import jax.numpy as jnp
from jax import lax
from jax.sharding import PartitionSpec as P

DEN = 256


def route_slots(expert_ids, gate_num, expert_count, capacity):
    tok_rows, route_count = expert_ids.shape
    routes = tok_rows * route_count
    flat_ids = expert_ids.reshape(-1)
    onehot = flat_ids[:, None] == jnp.arange(expert_count, dtype=jnp.int32)[None, :]
    order = jnp.arange(routes, dtype=jnp.int32)
    earlier = (order[None, :] < order[:, None]).astype(jnp.bfloat16)
    before = jnp.dot(earlier, onehot.astype(jnp.bfloat16), preferred_element_type=jnp.float32)
    route_rank = jnp.sum(jnp.where(onehot, before, 0.0), axis=1).astype(jnp.int32)
    slot = (flat_ids * capacity + route_rank).reshape(tok_rows, route_count)
    gate_values = gate_num.astype(jnp.float32) / DEN
    rows = jnp.arange(expert_count * capacity, dtype=jnp.int32)[:, None]
    hits = [rows == slot[None, :, k] for k in range(route_count)]
    placer = sum(h.astype(jnp.float32) for h in hits)
    weigher = sum(jnp.where(h, gate_values[None, :, k], 0.0) for k, h in enumerate(hits))
    return placer.astype(jnp.bfloat16), weigher.astype(jnp.bfloat16)


def exchange(rows, device_count, capacity):
    width = rows.shape[-1]
    blocks = rows.reshape(device_count, capacity * 4, width // 4)
    got = lax.all_to_all(blocks, ("dp", "expert"), split_axis=0, concat_axis=0, tiled=True)
    return got.reshape(device_count * capacity, width)


def on_device(tokens, expert_ids, gate_num, out_grad, gate_weight, up_weight, down_weight):
    device_count = lax.axis_size("dp") * lax.axis_size("expert")
    expert_count = device_count // 2
    tok_rows, route_count = expert_ids.shape
    capacity = 2 * ((3 * tok_rows * route_count + 4 * expert_count - 1) // (4 * expert_count))
    placer, weigher = route_slots(expert_ids, gate_num, expert_count, capacity)
    bf16, f32 = jnp.bfloat16, jnp.float32
    placer2 = jnp.concatenate([placer, placer], axis=0)
    weigher2 = jnp.concatenate([weigher, weigher], axis=0)
    x_rows = jnp.dot(placer2, tokens, preferred_element_type=f32).astype(bf16)
    g_rows = jnp.dot(weigher2, out_grad, preferred_element_type=f32).astype(bf16)
    rows_in = exchange(x_rows, device_count, capacity)
    grads_in = exchange(g_rows, device_count, capacity)
    gate_block, up_block, down_block = gate_weight[0], up_weight[0], down_weight[0]
    gate_act = jnp.dot(rows_in, gate_block, preferred_element_type=f32)
    up_act = jnp.dot(rows_in, up_block, preferred_element_type=f32)
    sigmoid_gate = jax.nn.sigmoid(gate_act)
    silu_gate = gate_act * sigmoid_gate
    hidden = (silu_gate * up_act).astype(bf16)
    partial_out = jnp.dot(hidden, down_block, preferred_element_type=f32).astype(bf16)
    out_back = exchange(partial_out, device_count, capacity)
    last = (((1,), (1,)), ((), ()))
    first = (((0,), (0,)), ((), ()))
    hidden_grad = lax.dot_general(grads_in, down_block, last, preferred_element_type=f32)
    up_grad_act = (hidden_grad * silu_gate).astype(bf16)
    gate_grad_act = (
        hidden_grad * up_act * sigmoid_gate * (1.0 + gate_act * (1.0 - sigmoid_gate))
    ).astype(bf16)
    row_part = lax.dot_general(gate_grad_act, gate_block, last, preferred_element_type=f32)
    row_part = row_part + lax.dot_general(
        up_grad_act, up_block, last, preferred_element_type=f32
    )
    row_back = exchange(row_part.astype(bf16), device_count, capacity)
    down_grad = lax.dot_general(hidden, grads_in, first, preferred_element_type=f32)
    gate_grad = lax.dot_general(rows_in, gate_grad_act, first, preferred_element_type=f32)
    up_grad = lax.dot_general(rows_in, up_grad_act, first, preferred_element_type=f32)
    moe_out = lax.dot_general(weigher2, out_back, first, preferred_element_type=f32)
    token_grad = lax.dot_general(placer2, row_back, first, preferred_element_type=f32)
    return (
        moe_out.astype(bf16),
        token_grad.astype(bf16),
        gate_grad.astype(bf16)[None],
        up_grad.astype(bf16)[None],
        down_grad.astype(bf16)[None],
    )


def solution(mesh):
    rows = P(("dp", "expert"), None)
    blocks = P(("dp", "expert"), None, None)
    return jax.shard_map(
        on_device,
        mesh=mesh,
        in_specs=(rows, rows, rows, rows, blocks, blocks, blocks),
        out_specs=(rows, rows, blocks, blocks, blocks),
        check_vma=False,
    )
```

time: 816 us -> 410 us (0.50); the launches traced: 800 us -> 408 us
  waiting for transfers between devices: 570 us -> 205 us
  other arithmetic: 35.4 us -> 1.62 us
  local copies, waits for them, and re-layouts: 77.1 us -> 88.3 us
  starting transfers between devices: 42.5 us -> 32.2 us
    all_to_all x4, waiting for transfers between devices: 570 us -> 205 us  [exchange(): lax.all_to_all(blocks, ('dp', 'expert'), split_axis=0, concat_axis=0, til...]
    reshape x5 -> x8, local copies, waits for them, and re-layouts: 45.6 us -> 86.2 us  [the longest x4 43.1 us: exchange(): return got.reshape(device_count * capacity, width)]
    dot_general x2 -> x0, local copies, waits for them, and re-layouts: 19.9 us -> none  [on_device(): jnp.dot(hidden, down_block, preferred_element_type=jnp.float32)]
    convert_element_type x3 -> x2, other arithmetic: 17.1 us -> 0.08 us  [the longest x1 0.08 us: route_slots(): return (placer.astype(jnp.bfloat16), weigher.astype(jnp.bfloat16))]
    concatenate x2 -> x0, other arithmetic: 16.7 us -> none  [the longest x1 8.38 us: on_device(): send_grads = jnp.concatenate([g_slots, g_slots], axis=0)]
    all_to_all x4, starting transfers between devices: 42.5 us -> 32.2 us  [exchange(): lax.all_to_all(blocks, ('dp', 'expert'), split_axis=0, concat_axis=0, til...]
    convert_element_type x2, local copies, waits for them, and re-layouts: 9.89 us -> 0.19 us  [route_slots(): jnp.sum(jnp.where(onehot, before, 0.0), axis=1).astype(jnp.int32)]
    dot_general x13 -> x14, matrix products: 73.9 us -> 80 us  [the longest x1 8.27 us: on_device(): up_act = jnp.dot(rows_in, up_block, preferred_element_type=f32)]
  transfers between devices with their start and end apart: 4 -> 4, of which waited for: 4 -> 4; matrix products, arithmetic and copies ran while one was open for 13% -> 24% of each run, Pallas kernels for 0% -> 0%
where the time goes in v1:
time: 410 us; the launch traced here: 408 us
  waiting for transfers between devices  205 us (50%)
  local copies, waits for them, and re-layouts  88.3 us (22%)
  matrix products  80 us (20%)
  starting transfers between devices  32.2 us (8%)
    all_to_all x4, waiting for transfers between devices, exchange(): lax.all_to_all(blocks, ('dp', 'expert'), split_axis=0, concat_axis=0, til...  205 us
    reshape x4, local copies, waits for them, and re-layouts, exchange(): return got.reshape(device_count * capacity, width)  43.1 us
    reshape x4, local copies, waits for them, and re-layouts, exchange(): blocks = rows.reshape(device_count, capacity * 4, width // 4)  43.1 us
    all_to_all x4, starting transfers between devices, exchange(): lax.all_to_all(blocks, ('dp', 'expert'), split_axis=0, concat_axis=0, til...  32.2 us
    dot_general x1, matrix products, on_device(): up_act = jnp.dot(rows_in, up_block, preferred_element_type=f32)  8.27 us
    dot_general x1, matrix products, on_device(): lax.dot_general(grads_in, down_block, last, preferred_element_type=f32)  8.21 us
  transfers between devices with their start and end apart: 4, of which 4 were waited for; matrix products, arithmetic and copies ran while one was open for 24% of the time, Pallas kernels for 0%

profile of v1, /device:TPU:1, one launch (start us, length us, event | category | flops | bytes accessed | tf_op | source)
XLA Modules:
  0.0 407.5 jit_solution(978361996532259619)
XLA Ops:
  0.6 0.8 convert_multiply_fusion
  1.5 0.9 copy.18
  3.7 5.6 %convolution_convert_fusion.1 = bf16[768,4096]{1,0:T(8,128)(2,1)} fusion(bf16[128,4096]{1,0:T(8,128)(2,1)} %param.7, bf16[384,128]{1,0:T(8,128)(2,1)S(1)} %get-tuple-element.9), kind=kOutput, calls=%fused_computation.2 | convolution fusion | flops 808845312 | bytes 7438336 | tf_op jit(solution)/shard_map/dot_general | solution.py:43
  9.4 10.7 %reshape.43 = bf16[128,24,1024]{2,1,0:T(8,128)(2,1)} reshape(bf16[768,4096]{1,0:T(8,128)(2,1)} %convolution_convert_fusion.1) | data formatting | bytes 12582912 | tf_op jit(solution)/shard_map/reshape | solution.py:29
  20.1 11.9 %all-to-all-start = ((bf16[128,24,1024]{2,1,0:T(8,128)(2,1)}), bf16[128,24,1024]{2,1,0:T(8,128)(2,1)}, u32[]{:S(2)}, u32[]{:S(2)}) async-start(bf16[128,24,1024]{2,1,0:T(8,128)(2,1)} %reshape.43), calls=%async_computation | async-start | bytes 12582912 | tf_op jit(solution)/shard_map/all_to_all | solution.py:30
  32.0 5.6 %convolution_convert_fusion = bf16[768,4096]{1,0:T(8,128)(2,1)} fusion(bf16[128,4096]{1,0:T(8,128)(2,1)} %param.10, bf16[384,128]{1,0:T(8,128)(2,1)S(1)} %get-tuple-element.8), kind=kOutput, calls=%fused_computation.1 | convolution fusion | flops 808845312 | bytes 7438336 | tf_op jit(solution)/shard_map/dot_general | solution.py:44
  37.6 10.8 %reshape.47 = bf16[128,24,1024]{2,1,0:T(8,128)(2,1)} reshape(bf16[768,4096]{1,0:T(8,128)(2,1)} %convolution_convert_fusion) | data formatting | bytes 12582912 | tf_op jit(solution)/shard_map/reshape | solution.py:29
  48.4 59.5 %all-to-all-done = bf16[128,24,1024]{2,1,0:T(8,128)(2,1)} async-done(((bf16[128,24,1024]{2,1,0:T(8,128)(2,1)}), bf16[128,24,1024]{2,1,0:T(8,128)(2,1)}, u32[]{:S(2)}, u32[]{:S(2)}) %all-to-all-start) | async-done | bytes 6291488 | tf_op jit(solution)/shard_map/all_to_all | solution.py:30
  107.9 6.8 %all-to-all-start.2 = ((bf16[128,24,1024]{2,1,0:T(8,128)(2,1)}), bf16[128,24,1024]{2,1,0:T(8,128)(2,1)}, u32[]{:S(2)}, u32[]{:S(2)}) async-start(bf16[128,24,1024]{2,1,0:T(8,128)(2,1)} %reshape.47), calls=%async_computation.2 | async-start | bytes 12582912 | tf_op jit(solution)/shard_map/all_to_all | solution.py:30
  114.7 10.7 %reshape.44 = bf16[768,4096]{1,0:T(8,128)(2,1)} reshape(bf16[128,24,1024]{2,1,0:T(8,128)(2,1)} %all-to-all-done) | data formatting | bytes 12582912 | tf_op jit(solution)/shard_map/reshape | solution.py:31
  125.5 8.3 %fusion.7 = f32[768,384]{1,0:T(8,128)} fusion(bf16[768,4096]{1,0:T(8,128)(2,1)} %reshape.44, bf16[1,4096,384]{2,1,0:T(8,128)(2,1)} %param.12), kind=kOutput, calls=%fused_computation.16 | convolution fusion | flops 2415919104 | bytes 10616832 | tf_op jit(solution)/shard_map/dot_general | solution.py:49
  133.7 4.4 %fusion.11 = f32[768,384]{1,0:T(8,128)} fusion(bf16[768,4096]{1,0:T(8,128)(2,1)S(1)} %copy-done.2, bf16[1,4096,384]{2,1,0:T(8,128)(2,1)S(1)} %copy-done.3), kind=kOutput, calls=%fused_computation.20 | convolution fusion | flops 2415919104 | bytes 10616832 | tf_op jit(solution)/shard_map/dot_general | solution.py:48
  138.2 52.5 %all-to-all-done.2 = bf16[128,24,1024]{2,1,0:T(8,128)(2,1)} async-done(((bf16[128,24,1024]{2,1,0:T(8,128)(2,1)}), bf16[128,24,1024]{2,1,0:T(8,128)(2,1)}, u32[]{:S(2)}, u32[]{:S(2)}) %all-to-all-start.2) | async-done | bytes 6291488 | tf_op jit(solution)/shard_map/all_to_all | solution.py:30
  190.6 10.8 %reshape.48 = bf16[768,4096]{1,0:T(8,128)(2,1)} reshape(bf16[128,24,1024]{2,1,0:T(8,128)(2,1)} %all-to-all-done.2) | data formatting | bytes 12582912 | tf_op jit(solution)/shard_map/reshape | solution.py:31
  201.4 8.2 %multiply_convert_fusion = (bf16[768,384]{1,0:T(8,128)(2,1)}, bf16[768,384]{1,0:T(8,128)(2,1)}, bf16[768,384]{1,0:T(8,128)(2,1)S(1)}) fusion(f32[768,384]{1,0:T(8,128)} %fusion.11, f32[768,384]{1,0:T(8,128)} %fusion.7, bf16[768,4096]{1,0:T(8,128)(2,1)} %reshape.48, bf16[1,384,4096]{2,1,0:T(8,128)(2,1)S(1)} %copy-done), kind=kOutput, calls=%fused_computation.22 | convolution fusion | flops 2420342784 | bytes 13565952 | tf_op jit(solution)/shard_map/dot_general | solution.py:57
  209.6 0.8 copy-done.4
  210.4 5.2 %convolution_convert_fusion.2 = bf16[768,4096]{1,0:T(8,128)(2,1)} fusion(bf16[768,384]{1,0:T(8,128)(2,1)S(1)} %get-tuple-element.7, bf16[1,384,4096]{2,1,0:T(8,128)(2,1)S(1)} %copy-done), kind=kOutput, calls=%fused_computation.3 | convolution fusion | flops 2419064832 | bytes 10027008 | tf_op jit(solution)/shard_map/dot_general | solution.py:53
  215.7 10.8 %reshape.45 = bf16[128,24,1024]{2,1,0:T(8,128)(2,1)} reshape(bf16[768,4096]{1,0:T(8,128)(2,1)} %convolution_convert_fusion.2) | data formatting | bytes 12582912 | tf_op jit(solution)/shard_map/reshape | solution.py:29
  226.5 6.8 %all-to-all-start.1 = ((bf16[128,24,1024]{2,1,0:T(8,128)(2,1)}), bf16[128,24,1024]{2,1,0:T(8,128)(2,1)}, u32[]{:S(2)}, u32[]{:S(2)}) async-start(bf16[128,24,1024]{2,1,0:T(8,128)(2,1)} %reshape.45), calls=%async_computation.1 | async-start | bytes 12582912 | tf_op jit(solution)/shard_map/all_to_all | solution.py:30
  233.3 5.4 %fusion.9 = f32[768,4096]{1,0:T(8,128)S(1)} fusion(bf16[768,384]{1,0:T(8,128)(2,1)S(1)} %copy-done.6, bf16[1,4096,384]{2,1,0:T(8,128)(2,1)} %param.11), kind=kOutput, calls=%fused_computation.18 | convolution fusion | flops 2415919104 | bytes 16318464 | tf_op jit(solution)/shard_map/dot_general | solution.py:62
  238.7 7.3 %add_convert_fusion = bf16[768,4096]{1,0:T(8,128)(2,1)} fusion(f32[768,4096]{1,0:T(8,128)S(1)} %fusion.9, bf16[768,384]{1,0:T(8,128)(2,1)S(1)} %copy-done.7, bf16[1,4096,384]{2,1,0:T(8,128)(2,1)} %param.12), kind=kOutput, calls=%fused_computation | convolution fusion | flops 2422210560 | bytes 22609920 | tf_op jit(solution)/shard_map/dot_general | solution.py:63
  246.0 10.8 %reshape.49 = bf16[128,24,1024]{2,1,0:T(8,128)(2,1)} reshape(bf16[768,4096]{1,0:T(8,128)(2,1)} %add_convert_fusion) | data formatting | bytes 12582912 | tf_op jit(solution)/shard_map/reshape | solution.py:29
  256.7 52.4 %all-to-all-done.1 = bf16[128,24,1024]{2,1,0:T(8,128)(2,1)} async-done(((bf16[128,24,1024]{2,1,0:T(8,128)(2,1)}), bf16[128,24,1024]{2,1,0:T(8,128)(2,1)}, u32[]{:S(2)}, u32[]{:S(2)}) %all-to-all-start.1) | async-done | bytes 6291488 | tf_op jit(solution)/shard_map/all_to_all | solution.py:30
  309.2 6.8 %all-to-all-start.3 = ((bf16[128,24,1024]{2,1,0:T(8,128)(2,1)}), bf16[128,24,1024]{2,1,0:T(8,128)(2,1)}, u32[]{:S(2)}, u32[]{:S(2)}) async-start(bf16[128,24,1024]{2,1,0:T(8,128)(2,1)} %reshape.49), calls=%async_computation.3 | async-start | bytes 12582912 | tf_op jit(solution)/shard_map/all_to_all | solution.py:30
  316.0 7.3 %fusion.2 = bf16[1,384,4096]{2,1,0:T(8,128)(2,1)} fusion(bf16[768,384]{1,0:T(8,128)(2,1)S(1)} %copy-done.5, bf16[768,4096]{1,0:T(8,128)(2,1)} %reshape.48), kind=kOutput, calls=%fused_computation.9 | convolution fusion | flops 2417491968 | bytes 10027008 | tf_op jit(solution)/shard_map/dot_general | solution.py:67
  323.2 8.1 %fusion.1 = bf16[1,4096,384]{2,1,0:T(8,128)(2,1)} fusion(bf16[768,4096]{1,0:T(8,128)(2,1)} %reshape.44, bf16[768,384]{1,0:T(8,128)(2,1)S(1)} %copy-done.7), kind=kOutput, calls=%fused_computation.8 | convolution fusion | flops 2417491968 | bytes 10027008 | tf_op jit(solution)/shard_map/dot_general | solution.py:69
  331.3 4.9 %fusion = bf16[1,4096,384]{2,1,0:T(8,128)(2,1)} fusion(bf16[768,4096]{1,0:T(8,128)(2,1)S(1)} %bitcast.48, bf16[768,384]{1,0:T(8,128)(2,1)S(1)} %copy-done.6), kind=kOutput, calls=%fused_computation.7 | convolution fusion | flops 2417491968 | bytes 10027008 | tf_op jit(solution)/shard_map/dot_general | solution.py:68
  336.2 10.7 %reshape.46 = bf16[768,4096]{1,0:T(8,128)(2,1)} reshape(bf16[128,24,1024]{2,1,0:T(8,128)(2,1)} %all-to-all-done.1) | data formatting | bytes 12582912 | tf_op jit(solution)/shard_map/reshape | solution.py:31
  346.9 4.8 %convolution_convert_fusion.7 = bf16[128,4096]{1,0:T(8,128)(2,1)} fusion(bf16[768,4096]{1,0:T(8,128)(2,1)} %reshape.46, bf16[384,128]{1,0:T(8,128)(2,1)S(1)} %get-tuple-element.8), kind=kOutput, calls=%fused_computation.11 | convolution fusion | flops 806223872 | bytes 7438336 | tf_op jit(solution)/shard_map/dot_general | solution.py:70
  351.7 40.2 %all-to-all-done.3 = bf16[128,24,1024]{2,1,0:T(8,128)(2,1)} async-done(((bf16[128,24,1024]{2,1,0:T(8,128)(2,1)}), bf16[128,24,1024]{2,1,0:T(8,128)(2,1)}, u32[]{:S(2)}, u32[]{:S(2)}) %all-to-all-start.3) | async-done | bytes 6291488 | tf_op jit(solution)/shard_map/all_to_all | solution.py:30
  391.9 10.9 %reshape.50 = bf16[768,4096]{1,0:T(8,128)(2,1)} reshape(bf16[128,24,1024]{2,1,0:T(8,128)(2,1)} %all-to-all-done.3) | data formatting | bytes 12582912 | tf_op jit(solution)/shard_map/reshape | solution.py:31
  402.8 4.8 %convolution_convert_fusion.6 = bf16[128,4096]{1,0:T(8,128)(2,1)} fusion(bf16[768,4096]{1,0:T(8,128)(2,1)} %reshape.50, bf16[384,128]{1,0:T(8,128)(2,1)S(1)} %get-tuple-element.9), kind=kOutput, calls=%fused_computation.10 | convolution fusion | flops 806223872 | bytes 7438336 | tf_op jit(solution)/shard_map/dot_general | solution.py:71
  (29 shorter events, 1.4 us)
Async XLA Ops:
  0.6 200.8 %copy-start = (bf16[1,384,4096]{2,1,0:T(8,128)(2,1)S(1)}, bf16[1,384,4096]{2,1,0:T(8,128)(2,1)}, u32[]{:S(2)}) copy-start(bf16[1,384,4096]{2,1,0:T(8,128)(2,1)} %param.13) | copy-start | bytes 9437188
  20.1 87.8 %all-to-all-start = ((bf16[128,24,1024]{2,1,0:T(8,128)(2,1)}), bf16[128,24,1024]{2,1,0:T(8,128)(2,1)}, u32[]{:S(2)}, u32[]{:S(2)}) async-start(bf16[128,24,1024]{2,1,0:T(8,128)(2,1)} %reshape.43), calls=%async_computation | async-start | bytes 12582912 | tf_op jit(solution)/shard_map/all_to_all | solution.py:30
  107.9 82.7 %all-to-all-start.2 = ((bf16[128,24,1024]{2,1,0:T(8,128)(2,1)}), bf16[128,24,1024]{2,1,0:T(8,128)(2,1)}, u32[]{:S(2)}, u32[]{:S(2)}) async-start(bf16[128,24,1024]{2,1,0:T(8,128)(2,1)} %reshape.47), calls=%async_computation.2 | async-start | bytes 12582912 | tf_op jit(solution)/shard_map/all_to_all | solution.py:30
  125.5 8.3 %copy-start.2 = (bf16[768,4096]{1,0:T(8,128)(2,1)S(1)}, bf16[768,4096]{1,0:T(8,128)(2,1)}, u32[]{:S(2)}) copy-start(bf16[768,4096]{1,0:T(8,128)(2,1)} %reshape.44) | copy-start | bytes 18874372
  125.5 8.3 %copy-start.3 = (bf16[1,4096,384]{2,1,0:T(8,128)(2,1)S(1)}, bf16[1,4096,384]{2,1,0:T(8,128)(2,1)}, u32[]{:S(2)}) copy-start(bf16[1,4096,384]{2,1,0:T(8,128)(2,1)} %param.11) | copy-start | bytes 9437188
  209.6 0.8 copy-start.4
  226.5 6.8 %copy-start.6 = (bf16[768,384]{1,0:T(8,128)(2,1)S(1)}, bf16[768,384]{1,0:T(8,128)(2,1)}, u32[]{:S(2)}) copy-start(bf16[768,384]{1,0:T(8,128)(2,1)} %get-tuple-element.6) | copy-start | bytes 1769476
  226.5 82.7 %all-to-all-start.1 = ((bf16[128,24,1024]{2,1,0:T(8,128)(2,1)}), bf16[128,24,1024]{2,1,0:T(8,128)(2,1)}, u32[]{:S(2)}, u32[]{:S(2)}) async-start(bf16[128,24,1024]{2,1,0:T(8,128)(2,1)} %reshape.45), calls=%async_computation.1 | async-start | bytes 12582912 | tf_op jit(solution)/shard_map/all_to_all | solution.py:30
  233.3 5.4 %copy-start.7 = (bf16[768,384]{1,0:T(8,128)(2,1)S(1)}, bf16[768,384]{1,0:T(8,128)(2,1)}, u32[]{:S(2)}) copy-start(bf16[768,384]{1,0:T(8,128)(2,1)} %get-tuple-element.5) | copy-start | bytes 1769476
  256.7 59.2 %copy-start.5 = (bf16[768,384]{1,0:T(8,128)(2,1)S(1)}, bf16[768,384]{1,0:T(8,128)(2,1)}, u32[]{:S(2)}) copy-start(bf16[768,384]{1,0:T(8,128)(2,1)} %copy-done.4) | copy-start | bytes 1769476
  309.2 82.7 %all-to-all-start.3 = ((bf16[128,24,1024]{2,1,0:T(8,128)(2,1)}), bf16[128,24,1024]{2,1,0:T(8,128)(2,1)}, u32[]{:S(2)}, u32[]{:S(2)}) async-start(bf16[128,24,1024]{2,1,0:T(8,128)(2,1)} %reshape.49), calls=%async_computation.3 | async-start | bytes 12582912 | tf_op jit(solution)/shard_map/all_to_all | solution.py:30
  316.0 15.3 %slice-start = ((s8[6291456]{0:T(1024)(128)(4,1)}), s8[4194304]{0:T(1024)(128)(4,1)S(1)}, s32[]{:S(2)}) async-start(s8[6291456]{0:T(1024)(128)(4,1)} %bitcast.47), calls=%async_computation.4 | async-start | bytes 8388608
  323.2 8.1 %slice-start.1 = ((s8[6291456]{0:T(1024)(128)(4,1)}), s8[2097152]{0:T(1024)(128)(4,1)S(1)}, s32[]{:S(2)}) async-start(s8[6291456]{0:T(1024)(128)(4,1)} %bitcast.47), calls=%async_computation.5 | async-start | bytes 4194304
  391.9 15.7 %copy-start.1 = (bf16[1,384,4096]{2,1,0:T(8,128)(2,1)S(1)}, bf16[1,384,4096]{2,1,0:T(8,128)(2,1)}, u32[]{:S(2)}) copy-start(bf16[1,384,4096]{2,1,0:T(8,128)(2,1)} %param.13) | copy-start | bytes 9437188

commit v2 on v1

v2 whole, which is shorter than its diff:
```python
import jax
import jax.numpy as jnp
from jax import lax
from jax.experimental import pallas as pl
from jax.experimental.pallas import tpu as pltpu
from jax.sharding import PartitionSpec as P

DEN = 256
MESH = pl.DeviceIdType.MESH
BF16, F32 = jnp.bfloat16, jnp.float32
CHUNKS = 2
PLANE = ((0, 1), (1, 0), (0, 3), (3, 0), (2, 2), (1, 1), (3, 3), (1, 3), (3, 1), (0, 2), (2, 0),
         (1, 2), (3, 2), (2, 1), (2, 3))
DPS = ((1, 0), (3, 0), (2, 0), (1, 1), (3, 1), (2, 1), (0, 1))


def place():
    dp, ex = lax.axis_index("dp"), lax.axis_index("expert")
    return dp // 2, dp % 2, ex // 4, ex % 4


def span(start, size):
    return pl.ds(pl.multiple_of(start, 16), size)


def remote(src, dst, s, r, yy, cc, xx, zz):
    return pltpu.make_async_remote_copy(
        src_ref=src, dst_ref=dst, send_sem=s, recv_sem=r,
        device_id=(yy * 2 + cc, xx * 4 + zz), device_id_type=MESH)


def dispatch(xs, og, wts, pi, spread, x_out, g_out, wbig, a1r, a2s, ogr, wr, b2s, a1_s, a1_r,
             b1_s, b1_r, sb_s, sb_r, w_s, w_r, a2_s, a2_r, b2_s, b2_r, l_s):
    y, c, x, z = place()
    dp, ex = y * 2 + c, x * 4 + z
    half = og.shape[1] // 2
    fold = half // CHUNKS
    wide = og.shape[1] // CHUNKS
    me = c * 4 + y
    own = [
        pltpu.make_async_copy(xs.at[span(ex * 48, 48)], a1r.at[span(ex * 48, 48)], l_s.at[0]),
        pltpu.make_async_copy(og, ogr.at[span(me * 128, 128)], l_s.at[1]),
        pltpu.make_async_copy(wts.at[span(dp % 4 * 96, 96)], wr.at[me], l_s.at[2]),
    ]
    for o in own:
        o.start()
    w_cp = []
    for d, dc in DPS:
        yy, cc = (y + d) % 4, (c + dc) % 2
        w_cp.append(remote(wts.at[span((yy * 2 + cc) % 4 * 96, 96)], wr.at[me],
                           w_s.at[d * 2 + dc], w_r.at[d * 2 + dc], yy, cc, x, z))
        w_cp[-1].start()
    a1, b1, sb, a2, b2, last = [], [], [], [], [], []
    for k in range(CHUNKS):
        thin, cols = pl.ds(k * fold, fold), pl.ds(k * wide, wide)
        b1.append([remote(og.at[:, cols], ogr.at[span(me * 128, 128), cols],
                          b1_s.at[k, d], b1_r.at[k, d], (y + d) % 4, c, x, z) for d in (1, 3, 2)])
        sb.append([remote(og.at[:, cols], ogr.at[span(me * 128, 128), cols],
                          sb_s.at[k, 0], sb_r.at[k, 0], y, 1 - c, x, z)])
        a1.append([])
        for dx, dz in PLANE:
            xx, zz = (x + dx) % 4, (z + dz) % 4
            a1[k].append(remote(
                xs.at[span((xx * 4 + zz) * 48, 48), thin], a1r.at[span(ex * 48, 48), thin],
                a1_s.at[k, dx * 4 + dz], a1_r.at[k, dx * 4 + dz], y, c, xx, zz))
        for cp in b1[k] + sb[k] + a1[k]:
            cp.start()
    for o in own:
        o.wait()
    for w in w_cp:
        w.wait_recv()
    for s in range(8):
        wbig[:, s * 128:(s + 1) * 128] = jnp.dot(
            spread[s], wr[s], preferred_element_type=F32).astype(BF16)
    for k in range(CHUNKS):
        thin, cols = pl.ds(k * fold, fold), pl.ds(k * wide, wide)
        for d, cp in zip((1, 3, 2), b1[k]):
            cp.wait_recv()
            block = ogr.at[span((c * 4 + (y + 4 - d) % 4) * 128, 128), cols]
            sb[k].append(remote(block, block, sb_s.at[k, d], sb_r.at[k, d], y, 1 - c, x, z))
            sb[k][-1].start()
        for cp in a1[k]:
            cp.wait_recv()
        a2.append([])
        for dy in (1, 0):
            for dc in (0, 1):
                cc = (c + dc) % 2
                q = ((y + dy) % 2) * 2 + cc
                for h in range(2):
                    part = pl.ds(h * half + k * fold, fold)
                    a2s[span(q * 96, 96), part] = jnp.dot(
                        pi[span((q * 2 + h) * 96, 96), :], a1r[:, thin],
                        preferred_element_type=F32).astype(BF16)
                    for far in (0, 2):
                        d = dy + far
                        spot = x_out.at[span(dp * 96, 96), part]
                        if d == 0 and dc == 0:
                            cp = pltpu.make_async_copy(
                                a2s.at[span(q * 96, 96), part], spot, l_s.at[3 + k * 2 + h])
                            last.append(cp)
                        else:
                            n = (d * 2 + dc) * 2 + h
                            cp = remote(a2s.at[span(q * 96, 96), part], spot, a2_s.at[k, n],
                                        a2_r.at[k, n], (y + d) % 4, cc, x, z)
                            a2[k].append(cp)
                        cp.start()
        for cp in sb[k]:
            cp.wait_recv()
        for h in range(4):
            band = pl.ds(h * 192, 192)
            b2s[band, cols] = jnp.dot(
                wbig[band, :], ogr[:, cols], preferred_element_type=F32).astype(BF16)
        b2.append([])
        spot = g_out.at[span(ex * 48, 48), cols]
        for dx, dz in PLANE:
            xx, zz = (x + dx) % 4, (z + dz) % 4
            n = dx * 4 + dz
            b2[k].append(remote(b2s.at[span((xx * 4 + zz) * 48, 48), cols], spot,
                                b2_s.at[k, n], b2_r.at[k, n], y, c, xx, zz))
            b2[k][-1].start()
        last.append(pltpu.make_async_copy(b2s.at[span(ex * 48, 48), cols], spot, l_s.at[7 + k]))
        last[-1].start()
    for k in range(CHUNKS):
        for cp in a2[k] + b2[k]:
            cp.wait_recv()
    for cp in last:
        cp.wait()
    for cp in w_cp + sum(a1 + b1 + sb + a2 + b2, []):
        cp.wait_send()


def homeward(out_b, row_a, wbig_t, pi_t, placer_t, moe, tok, br, ar, tot, part, sibr, partr, back,
             backr, c1_s, c1_r, d1_s, d1_r, sb_s, sb_r, c2_s, c2_r, d2_s, d2_r, l_s):
    y, c, x, z = place()
    dp, ex = y * 2 + c, x * 4 + z
    half = out_b.shape[1] // 2
    fold = half // CHUNKS
    wide = out_b.shape[1] // CHUNKS
    c1, d1, sb, c2, d2, own1, own2 = [], [], [], [], [], [], []
    for k in range(CHUNKS):
        cols = pl.ds(k * wide, wide)
        own1.append([pltpu.make_async_copy(
            out_b.at[span(ex * 48, 48), cols], br.at[span(ex * 48, 48), cols], l_s.at[k])])
        d1.append([])
        for h in range(2):
            piece = pl.ds(h * half + k * fold, fold)
            own1[k].append(pltpu.make_async_copy(
                row_a.at[span(dp * 96, 96), piece], ar.at[span(dp * 96, 96), piece],
                l_s.at[2 + k * 2 + h]))
            for d, dc in DPS:
                yy, cc = (y + d) % 4, (c + dc) % 2
                n = (d * 2 + dc) * 2 + h
                d1[k].append(remote(
                    row_a.at[span((yy * 2 + cc) * 96, 96), piece],
                    ar.at[span(dp * 96, 96), piece], d1_s.at[k, n], d1_r.at[k, n], yy, cc, x, z))
        c1.append([])
        for dx, dz in PLANE:
            xx, zz = (x + dx) % 4, (z + dz) % 4
            n = dx * 4 + dz
            c1[k].append(remote(
                out_b.at[span((xx * 4 + zz) * 48, 48), cols], br.at[span(ex * 48, 48), cols],
                c1_s.at[k, n], c1_r.at[k, n], y, c, xx, zz))
        for cp in own1[k] + d1[k] + c1[k]:
            cp.start()
    for k in range(CHUNKS):
        thin, cols = pl.ds(k * fold, fold), pl.ds(k * wide, wide)
        for cp in own1[k]:
            cp.wait()
        for cp in c1[k]:
            cp.wait_recv()
        for s in range(4):
            band = pl.ds(s * 256, 256)
            part[band, cols] = jnp.dot(
                wbig_t[band, :], br[:, cols], preferred_element_type=F32).astype(BF16)
        sb.append(remote(part.at[span((1 - c) * 512, 512), cols], sibr.at[:, cols],
                         sb_s.at[k], sb_r.at[k], y, 1 - c, x, z))
        sb[k].start()
        for cp in d1[k]:
            cp.wait_recv()
        for q in range(4):
            for h in range(2):
                piece = pl.ds(h * half + k * fold, fold)
                tot[(q * 2 + h) * 96:(q * 2 + h + 1) * 96, :] = (
                    ar[q * 96:(q + 1) * 96, piece].astype(F32)
                    + ar[384 + q * 96:384 + (q + 1) * 96, piece].astype(F32)).astype(BF16)
        for h in range(4):
            band = pl.ds(h * 192, 192)
            back[band, thin] = jnp.dot(
                pi_t[band, :], tot[...], preferred_element_type=F32).astype(BF16)
        d2.append([])
        for dx, dz in PLANE:
            xx, zz = (x + dx) % 4, (z + dz) % 4
            n = dx * 4 + dz
            d2[k].append(remote(
                back.at[span((xx * 4 + zz) * 48, 48), thin], backr.at[span(ex * 48, 48), thin],
                d2_s.at[k, n], d2_r.at[k, n], y, c, xx, zz))
        own2.append([pltpu.make_async_copy(
            back.at[span(ex * 48, 48), thin], backr.at[span(ex * 48, 48), thin], l_s.at[6 + k])])
        for cp in d2[k] + own2[k]:
            cp.start()
        sb[k].wait_recv()
        sibr[:, cols] = (part[span(c * 512, 512), cols].astype(F32)
                         + sibr[:, cols].astype(F32)).astype(BF16)
        c2.append([])
        spot = partr.at[span(y * 128, 128), cols]
        for d in (1, 3, 2):
            yy = (y + d) % 4
            c2[k].append(remote(sibr.at[span(yy * 128, 128), cols], spot,
                                c2_s.at[k, d], c2_r.at[k, d], yy, c, x, z))
            c2[k][-1].start()
        own2[k].append(pltpu.make_async_copy(sibr.at[span(y * 128, 128), cols], spot,
                                             l_s.at[8 + k]))
        own2[k][-1].start()
    for k in range(CHUNKS):
        thin, cols = pl.ds(k * fold, fold), pl.ds(k * wide, wide)
        for cp in own2[k]:
            cp.wait()
        for cp in c2[k] + d2[k]:
            cp.wait_recv()
        for h in range(2):
            tok[:, pl.ds(h * half + k * fold, fold)] = jnp.dot(
                placer_t[h], backr[:, thin], preferred_element_type=F32).astype(BF16)
        moe[:, cols] = sum(
            partr[s * 128:(s + 1) * 128, cols].astype(F32) for s in range(4)).astype(BF16)
    for cp in sum(c1 + d1 + c2 + d2, sb):
        cp.wait_send()


VM = pl.BlockSpec(memory_space=pltpu.VMEM)
HB = pl.BlockSpec(memory_space=pltpu.HBM)


def sems(*sizes):
    return [pltpu.SemaphoreType.DMA(s) for s in sizes for _ in (0, 1)]


def vm(*shape):
    return pltpu.VMEM(shape, BF16)


def out(*shape):
    return jax.ShapeDtypeStruct(shape, BF16)


def call_dispatch(xs, og, wts, pi, spread):
    w, k = og.shape[1], CHUNKS
    return pl.pallas_call(
        dispatch,
        out_shape=(out(768, w), out(768, w), out(768, 1024)),
        in_specs=[VM] * 5,
        out_specs=(HB, HB, VM),
        scratch_shapes=[
            vm(768, w // 2), vm(384, w), vm(1024, w), vm(8, 96, 128), vm(768, w),
            *sems((k, 16), (k, 4), (k, 4), (8,), (k, 16), (k, 16)),
            pltpu.SemaphoreType.DMA((9,))],
        compiler_params=pltpu.CompilerParams(has_side_effects=True, vmem_limit_bytes=56 << 20),
    )(xs, og, wts, pi, spread)


def call_homeward(out_b, row_a, wbig_t, pi_t, placer_t):
    w, k = out_b.shape[1], CHUNKS
    return pl.pallas_call(
        homeward,
        out_shape=(out(128, w), out(128, w)),
        in_specs=[HB, HB, VM, VM, VM],
        out_specs=(VM, VM),
        scratch_shapes=[
            vm(768, w), vm(768, w), vm(768, w // 2 // k), vm(1024, w), vm(512, w), vm(512, w),
            vm(768, w // 2), vm(768, w // 2),
            *sems((k, 16), (k, 16), (k,), (k, 4), (k, 16)), pltpu.SemaphoreType.DMA((10,))],
        compiler_params=pltpu.CompilerParams(has_side_effects=True, vmem_limit_bytes=58 << 20),
    )(out_b, row_a, wbig_t, pi_t, placer_t)


def one_hot(index, size):
    return (index[:, None] == jnp.arange(size, dtype=jnp.int32)[None, :]).astype(BF16)


def ranks(expert_ids, expert_count):
    tok_rows, route_count = expert_ids.shape
    flat = expert_ids.reshape(-1)
    hit = flat[:, None] == jnp.arange(expert_count, dtype=jnp.int32)[None, :]
    order = jnp.arange(tok_rows * route_count, dtype=jnp.int32)
    earlier = (order[None, :] < order[:, None]).astype(BF16)
    before = jnp.dot(earlier, hit.astype(BF16), preferred_element_type=F32)
    rank = jnp.sum(jnp.where(hit, before, 0.0), axis=1).astype(jnp.int32)
    return rank.reshape(tok_rows, route_count)


def to_b(a):
    return a.reshape(8, 16, 6, -1).transpose(1, 0, 2, 3).reshape(768, -1)


def to_a(b):
    return b.reshape(16, 8, 6, -1).transpose(1, 0, 2, 3).reshape(768, -1)


def on_device(tokens, expert_ids, gate_num, out_grad, gate_weight, up_weight, down_weight):
    rank = ranks(expert_ids, 64)
    gate = gate_num.astype(F32) / DEN
    rows = jnp.arange(384, dtype=jnp.int32)[:, None]
    slot_b = expert_ids * 6 + rank
    wts = sum(jnp.where(rows == slot_b[None, :, k], gate[None, :, k], 0.0) for k in (0, 1))
    slot_a = (expert_ids % 16) * 48 + (expert_ids // 16) * 6 + rank
    rows = jnp.arange(768, dtype=jnp.int32)[:, None]
    placer = [
        sum((rows == slot_a[None, :, k] + h * 24).astype(F32) for k in (0, 1)).astype(BF16)
        for h in (0, 1)
    ]
    half = tokens.shape[1] // 2
    folded = jnp.concatenate([tokens[:, :half], tokens[:, half:]], axis=0)
    xs = jnp.dot(
        jnp.concatenate(placer, axis=1), folded, preferred_element_type=F32).astype(BF16)
    j = jnp.arange(768, dtype=jnp.int32)
    pi = one_hot(j % 96 // 6 * 48 + j // 96 % 2 * 24 + j // 192 * 6 + j % 6, 768)
    home = j // 48 * 6 + j % 6
    source = j % 48 // 6
    spread = jnp.stack([
        one_hot(jnp.where(source == s % 4 * 2 + s // 4, home, -1), 96) for s in range(8)])
    rows_in, grads_in, wbig = call_dispatch(xs, out_grad, wts.astype(BF16), pi, spread)
    gate_block, up_block, down_block = gate_weight[0], up_weight[0], down_weight[0]
    gate_act = jnp.dot(rows_in, gate_block, preferred_element_type=F32)
    up_act = jnp.dot(rows_in, up_block, preferred_element_type=F32)
    sigmoid_gate = jax.nn.sigmoid(gate_act)
    silu_gate = gate_act * sigmoid_gate
    hidden = to_b((silu_gate * up_act).astype(BF16))
    out_b = jnp.dot(hidden, down_block, preferred_element_type=F32).astype(BF16)
    last = (((1,), (1,)), ((), ()))
    first = (((0,), (0,)), ((), ()))
    hidden_grad = to_a(lax.dot_general(grads_in, down_block, last, preferred_element_type=F32))
    up_grad_act = (hidden_grad * silu_gate).astype(BF16)
    gate_grad_act = (
        hidden_grad * up_act * sigmoid_gate * (1.0 + gate_act * (1.0 - sigmoid_gate))
    ).astype(BF16)
    row_part = lax.dot_general(gate_grad_act, gate_block, last, preferred_element_type=F32)
    row_part = row_part + lax.dot_general(
        up_grad_act, up_block, last, preferred_element_type=F32
    )
    moe_out, token_grad = call_homeward(
        out_b, row_part.astype(BF16), wbig.T, pi.T, jnp.stack([p.T for p in placer]))
    down_grad = lax.dot_general(hidden, grads_in, first, preferred_element_type=F32)
    gate_grad = lax.dot_general(rows_in, gate_grad_act, first, preferred_element_type=F32)
    up_grad = lax.dot_general(rows_in, up_grad_act, first, preferred_element_type=F32)
    return (
        moe_out,
        token_grad,
        gate_grad.astype(BF16)[None],
        up_grad.astype(BF16)[None],
        down_grad.astype(BF16)[None],
    )


def solution(mesh):
    rows = P(("dp", "expert"), None)
    blocks = P(("dp", "expert"), None, None)
    return jax.shard_map(
        on_device,
        mesh=mesh,
        in_specs=(rows, rows, rows, rows, blocks, blocks, blocks),
        out_specs=(rows, rows, blocks, blocks, blocks),
        check_vma=False,
    )
```

time: 410 us -> 387 us (0.944)
  Pallas kernels: 0 us -> 275 us
  waiting for transfers between devices: 205 us -> 0 us
  local copies, waits for them, and re-layouts: 88.3 us -> 26.6 us
  starting transfers between devices: 32.2 us -> 0 us
  matrix products: 80 us -> 72 us
  other arithmetic: 1.62 us -> 8.41 us
    pallas_call x0 -> x2, Pallas kernels: none -> 275 us  [the longest x1 138 us: call_homeward(): pl.pallas_call(homeward, out_shape=(out(128, w), out(128, w)), in_specs=[...]
    all_to_all x4 -> x0, waiting for transfers between devices: 205 us -> none  [exchange(): lax.all_to_all(blocks, ('dp', 'expert'), split_axis=0, concat_axis=0, til...]
    reshape x8 -> x3, local copies, waits for them, and re-layouts: 86.2 us -> 6.51 us  [the longest x2 4.08 us: to_b(): return a.reshape(8, 16, 6, -1).transpose(1, 0, 2, 3).reshape(768, -1)]
    all_to_all x4 -> x0, starting transfers between devices: 32.2 us -> none  [exchange(): lax.all_to_all(blocks, ('dp', 'expert'), split_axis=0, concat_axis=0, til...]
    dot_general x0 -> x1, local copies, waits for them, and re-layouts: none -> 10.1 us  [on_device(): lax.dot_general(grads_in, down_block, last, preferred_element_type=F32)]
    dot_general x14 -> x11, matrix products: 80 us -> 72 us  [the longest x1 10 us: on_device(): lax.dot_general(grads_in, down_block, last, preferred_element_type=F32)]
  transfers between devices with their start and end apart: 4 -> 0, of which waited for: 4 -> 0; matrix products, arithmetic and copies ran while one was open for 24% -> 0% of each run, Pallas kernels for 0% -> 0%
where the time goes in v2:
time: 387 us; the launch traced here: 383 us
  Pallas kernels  275 us (71%)
  matrix products  72 us (19%)
  local copies, waits for them, and re-layouts  26.6 us (7%)
  other arithmetic  8.41 us (2%)
    pallas_call x1, Pallas kernels, call_homeward(): pl.pallas_call(homeward, out_shape=(out(128, w), out(128, w)), in_specs=[...  138 us
    pallas_call x1, Pallas kernels, call_dispatch(): pl.pallas_call(dispatch, out_shape=(out(768, w), out(768, w), out(768, 10...  136 us
    dot_general x1, local copies, waits for them, and re-layouts, on_device(): lax.dot_general(grads_in, down_block, last, preferred_element_type=F32)  10.1 us
    dot_general x1, matrix products, on_device(): lax.dot_general(grads_in, down_block, last, preferred_element_type=F32)  10 us
    dot_general x1, matrix products, on_device(): lax.dot_general(up_grad_act, up_block, last, preferred_element_type=F32)  8.73 us
    dot_general x1, matrix products, on_device(): gate_act = jnp.dot(rows_in, gate_block, preferred_element_type=F32)  8.51 us
    dot_general x1, matrix products, on_device(): lax.dot_general(rows_in, up_grad_act, first, preferred_element_type=F32)  8.08 us
    dot_general x1, matrix products, on_device(): lax.dot_general(rows_in, gate_grad_act, first, preferred_element_type=F32)  7.99 us

profile of v2, /device:TPU:1, one launch (start us, length us, event | category | flops | bytes accessed | tf_op | source)
XLA Modules:
  0.0 382.8 jit_solution(18108595237072339169)
XLA Ops:
  0.6 0.9 copy.30
  1.7 0.2 fusion.19
  2.1 0.7 broadcast_multiply_fusion
  2.9 0.7 broadcast_compare_fusion
  3.8 0.2 slice_reduce_fusion.1
  4.2 1.3 fusion.83
  5.5 2.7 convolution_convert_fusion.4.xs
  8.2 0.7 add_convert_fusion.5.wts
  8.9 1.7 fusion.14
  11.1 0.2 fusion.28
  12.5 1.5 stack.7.spread
  14.0 136.3 %shard_map.110 = (bf16[768,4096]{1,0:T(8,128)(2,1)}, bf16[768,4096]{1,0:T(8,128)(2,1)}, bf16[768,1024]{1,0:T(8,128)(2,1)}) custom-call(bf16[768,2048]{1,0:T(8,128)(2,1)} %convolution_convert_fusion.4.xs, bf16[128,4096]{1,0:T(8,128)(2,1)} %og.1, bf16[384,128]{1,0:T(8,128)(2,1)} %add_convert_fusion.5.wts, bf16[768,768]{1,0:T(8,128)(2,1)} %get-tuple-element.27.pi, ...), custom_call_target="tpu_custom_call" | custom-call | tf_op jit(solution)/shard_map/pallas_call | solution.py:247
  150.4 6.8 %fusion.7 = f32[768,384]{1,0:T(8,128)} fusion(bf16[768,4096]{1,0:T(8,128)(2,1)} %get-tuple-element.10, bf16[1,4096,384]{2,1,0:T(8,128)(2,1)S(1)} %copy-done.3), kind=kOutput, calls=%fused_computation.13 | convolution fusion | flops 2415919104 | bytes 10616832 | tf_op jit(solution)/shard_map/dot_general | solution.py:323
  157.2 10.1 %dot_general.40 = bf16[16,8,6,4096]{3,2,1,0:T(8,128)(2,1)} reshape(bf16[768,4096]{1,0:T(8,128)(2,1)} %get-tuple-element.11) | data formatting | bytes 12582912 | tf_op jit(solution)/shard_map/dot_general | solution.py:330
  167.3 10.0 %fusion.15 = f32[8,16,6,384]{3,2,0,1:T(8,128)S(1)} fusion(bf16[16,8,6,4096]{3,2,1,0:T(8,128)(2,1)} %dot_general.40, bf16[1,384,4096]{2,1,0:T(8,128)(2,1)} %param.13), kind=kOutput, calls=%fused_computation.23 | convolution fusion | flops 2415919104 | bytes 10616832 | tf_op jit(solution)/shard_map/dot_general | solution.py:330
  177.4 1.2 copy.40
  178.6 2.4 reshape.578
  181.0 8.5 %multiply_convert_fusion = (bf16[768,384]{1,0:T(8,128)(2,1)}, bf16[768,384]{1,0:T(8,128)(2,1)}, bf16[768,384]{1,0:T(8,128)(2,1)}) fusion(f32[768,384]{1,0:T(8,128)} %reshape.578, f32[768,384]{1,0:T(8,128)} %fusion.7, bf16[768,4096]{1,0:T(8,128)(2,1)} %get-tuple-element.10, bf16[1,4096,384]{2,1,0:T(8,128)(2,1)S(1)} %copy-done), kind=kOutput, calls=%fused_computation.24 | convolution fusion | flops 2420342784 | bytes 13565952 | tf_op jit(solution)/shard_map/dot_general | solution.py:322
  189.6 2.0 reshape.576
  191.6 2.1 copy.39
  193.7 2.0 reshape.577
  195.8 7.4 %fusion.2 = bf16[1,384,4096]{2,1,0:T(8,128)(2,1)} fusion(bf16[768,384]{1,0:T(8,128)(2,1)} %reshape.577, bf16[768,4096]{1,0:T(8,128)(2,1)} %get-tuple-element.11), kind=kOutput, calls=%fused_computation.7 | convolution fusion | flops 2417491968 | bytes 10027008 | tf_op jit(solution)/shard_map/dot_general | solution.py:341
  203.1 6.4 %fusion.9 = f32[768,4096]{1,0:T(8,128)} fusion(bf16[768,384]{1,0:T(8,128)(2,1)S(1)} %copy-done.10, bf16[1,4096,384]{2,1,0:T(8,128)(2,1)S(1)} %copy-done), kind=kOutput, calls=%fused_computation.15 | convolution fusion | flops 2415919104 | bytes 16318464 | tf_op jit(solution)/shard_map/dot_general | solution.py:335
  209.5 8.7 %add_convert_fusion.row_a = bf16[768,4096]{1,0:T(8,128)(2,1)} fusion(f32[768,4096]{1,0:T(8,128)} %fusion.9, bf16[768,384]{1,0:T(8,128)(2,1)S(1)} %copy-done.8, bf16[1,4096,384]{2,1,0:T(8,128)(2,1)S(1)} %copy-done.4), kind=kOutput, calls=%fused_computation | convolution fusion | flops 2422210560 | bytes 22609920 | tf_op jit(solution)/shard_map/dot_general | solution.py:336
  218.3 5.3 %convolution_convert_fusion.out_b = bf16[768,4096]{1,0:T(8,128)(2,1)} fusion(bf16[768,384]{1,0:T(8,128)(2,1)S(1)} %copy-done.2, bf16[1,384,4096]{2,1,0:T(8,128)(2,1)S(1)} %copy-done.13), kind=kOutput, calls=%fused_computation.1 | convolution fusion | flops 2419064832 | bytes 10027008 | tf_op jit(solution)/shard_map/dot_general | solution.py:327
  223.6 1.6 copy.41
  225.4 0.8 pad_maximum_fusion.placer_t
  226.2 138.4 %shard_map.111 = (bf16[128,4096]{1,0:T(8,128)(2,1)}, bf16[128,4096]{1,0:T(8,128)(2,1)}) custom-call(bf16[768,4096]{1,0:T(8,128)(2,1)} %convolution_convert_fusion.out_b, bf16[768,4096]{1,0:T(8,128)(2,1)} %add_convert_fusion.row_a, bf16[1024,768]{1,0:T(8,128)(2,1)} %bitcast.49, bf16[768,768]{1,0:T(8,128)(2,1)} %get-tuple-element.26.pi_t, ...), custom_call_target="tpu_custom_call" | custom-call | tf_op jit(solution)/shard_map/pallas_call | solution.py:262
  364.6 8.0 %fusion = bf16[1,4096,384]{2,1,0:T(8,128)(2,1)} fusion(bf16[768,4096]{1,0:T(8,128)(2,1)} %get-tuple-element.10, bf16[768,384]{1,0:T(8,128)(2,1)S(1)} %copy-done.11), kind=kOutput, calls=%fused_computation.5 | convolution fusion | flops 2417491968 | bytes 10027008 | tf_op jit(solution)/shard_map/dot_general | solution.py:342
  372.6 8.1 %fusion.1 = bf16[1,4096,384]{2,1,0:T(8,128)(2,1)} fusion(bf16[768,4096]{1,0:T(8,128)(2,1)} %get-tuple-element.10, bf16[768,384]{1,0:T(8,128)(2,1)S(1)} %copy-done.9), kind=kOutput, calls=%fused_computation.6 | convolution fusion | flops 2417491968 | bytes 10027008 | tf_op jit(solution)/shard_map/dot_general | solution.py:343
  380.7 1.0 copy.52
  381.6 1.0 copy.53
  (58 shorter events, 2.8 us)
Async XLA Ops:
  0.6 180.4 %copy-start = (bf16[1,4096,384]{2,1,0:T(8,128)(2,1)S(1)}, bf16[1,4096,384]{2,1,0:T(8,128)(2,1)}, u32[]{:S(2)}) copy-start(bf16[1,4096,384]{2,1,0:T(8,128)(2,1)} %param.11) | copy-start | bytes 9437188
  5.5 2.7 copy-start.12
  14.0 136.4 %copy-start.3 = (bf16[1,4096,384]{2,1,0:T(8,128)(2,1)S(1)}, bf16[1,4096,384]{2,1,0:T(8,128)(2,1)}, u32[]{:S(2)}) copy-start(bf16[1,4096,384]{2,1,0:T(8,128)(2,1)} %param.12) | copy-start | bytes 9437188
  195.8 7.4 %copy-start.10 = (bf16[768,384]{1,0:T(8,128)(2,1)S(1)}, bf16[768,384]{1,0:T(8,128)(2,1)}, u32[]{:S(2)}) copy-start(bf16[768,384]{1,0:T(8,128)(2,1)} %get-tuple-element.20) | copy-start | bytes 1769476
  203.1 6.4 %copy-start.4 = (bf16[1,4096,384]{2,1,0:T(8,128)(2,1)S(1)}, bf16[1,4096,384]{2,1,0:T(8,128)(2,1)}, u32[]{:S(2)}) copy-start(bf16[1,4096,384]{2,1,0:T(8,128)(2,1)} %param.12) | copy-start | bytes 9437188
  203.1 6.4 %copy-start.8 = (bf16[768,384]{1,0:T(8,128)(2,1)S(1)}, bf16[768,384]{1,0:T(8,128)(2,1)}, u32[]{:S(2)}) copy-start(bf16[768,384]{1,0:T(8,128)(2,1)} %get-tuple-element.19) | copy-start | bytes 1769476
  209.5 8.7 %copy-start.2 = (bf16[768,384]{1,0:T(8,128)(2,1)S(1)}, bf16[768,384]{1,0:T(8,128)(2,1)}, u32[]{:S(2)}) copy-start(bf16[768,384]{1,0:T(8,128)(2,1)} %reshape.577) | copy-start | bytes 1769476
  209.5 8.7 %copy-start.13 = (bf16[1,384,4096]{2,1,0:T(8,128)(2,1)S(1)}, bf16[1,384,4096]{2,1,0:T(8,128)(2,1)}, u32[]{:S(2)}) copy-start(bf16[1,384,4096]{2,1,0:T(8,128)(2,1)} %param.13) | copy-start | bytes 9437188
  218.2 5.3 %copy-start.5 = (bf16[768,1024]{1,0:T(8,128)(2,1)S(1)}, bf16[768,1024]{1,0:T(8,128)(2,1)}, u32[]{:S(2)}) copy-start(bf16[768,1024]{1,0:T(8,128)(2,1)} %get-tuple-element.12) | copy-start | bytes 4718596
  226.2 138.4 %copy-start.11 = (bf16[768,384]{1,0:T(8,128)(2,1)S(1)}, bf16[768,384]{1,0:T(8,128)(2,1)}, u32[]{:S(2)}) copy-start(bf16[768,384]{1,0:T(8,128)(2,1)} %get-tuple-element.20) | copy-start | bytes 1769476
  364.6 8.0 %copy-start.9 = (bf16[768,384]{1,0:T(8,128)(2,1)S(1)}, bf16[768,384]{1,0:T(8,128)(2,1)}, u32[]{:S(2)}) copy-start(bf16[768,384]{1,0:T(8,128)(2,1)} %get-tuple-element.19) | copy-start | bytes 1769476
  372.6 8.1 %copy-start.7 = (bf16[128,4096]{1,0:T(8,128)(2,1)S(1)}, bf16[128,4096]{1,0:T(8,128)(2,1)}, u32[]{:S(2)}) copy-start(bf16[128,4096]{1,0:T(8,128)(2,1)} %get-tuple-element.37) | copy-start | bytes 3145732
  372.6 9.1 %copy-start.6 = (bf16[128,4096]{1,0:T(8,128)(2,1)S(1)}, bf16[128,4096]{1,0:T(8,128)(2,1)}, u32[]{:S(2)}) copy-start(bf16[128,4096]{1,0:T(8,128)(2,1)} %get-tuple-element.38) | copy-start | bytes 3145732
  372.6 10.0 %copy-start.1 = (bf16[1,4096,384]{2,1,0:T(8,128)(2,1)S(1)}, bf16[1,4096,384]{2,1,0:T(8,128)(2,1)}, u32[]{:S(2)}) copy-start(bf16[1,4096,384]{2,1,0:T(8,128)(2,1)} %param.11) | copy-start | bytes 9437188

commit v3 on v2

--- a/solution.py
+++ b/solution.py
@@ -129,101 +129,227 @@
         cp.wait_send()
 
 
-def homeward(out_b, row_a, wbig_t, pi_t, placer_t, moe, tok, br, ar, tot, part, sibr, partr, back,
-             backr, c1_s, c1_r, d1_s, d1_r, sb_s, sb_r, c2_s, c2_r, d2_s, d2_r, l_s):
+def experts(rows_in, grads_in, gate_w, up_w, down_w, wbig_t, pi_t, placer_t, pab, pba,
+            moe, tok, gate_g, up_g, down_g, br, ar, sibr,
+            out_b, row_a, partr, backr,
+            c1_s, c1_r, d1_s, d1_r, sb_s, sb_r, c2_s, c2_r, d2_s, d2_r, l_s):
     y, c, x, z = place()
     dp, ex = y * 2 + c, x * 4 + z
     half = out_b.shape[1] // 2
     fold = half // CHUNKS
     wide = out_b.shape[1] // CHUNKS
-    c1, d1, sb, c2, d2, own1, own2 = [], [], [], [], [], [], []
-    for k in range(CHUNKS):
+    last = (((1,), (1,)), ((), ()))
+    first = (((0,), (0,)), ((), ()))
+
+    def c1_copies(k, dx):
+        cols, xx = pl.ds(k * wide, wide), (x + dx) % 4
+        made = []
+        for dz in (1, 3, 2, 0):
+            zz = (z + dz) % 4
+            n = dx * 4 + dz
+            if n:
+                made.append(remote(
+                    out_b.at[span((xx * 4 + zz) * 48, 48), cols], br.at[span(ex * 48, 48), cols],
+                    c1_s.at[k, n], c1_r.at[k, n], y, c, xx, zz))
+        return made
+
+    def d1_copies(k, h):
+        piece = pl.ds(h * half + k * fold, fold)
+        made = []
+        for d, dc in DPS:
+            yy, cc = (y + d) % 4, (c + dc) % 2
+            n = (d * 2 + dc) * 2 + h
+            made.append(remote(
+                row_a.at[span((yy * 2 + cc) * 96, 96), piece], ar.at[span(dp * 96, 96), piece],
+                d1_s.at[k, n], d1_r.at[k, n], yy, cc, x, z))
+        return made
+
+    def own_out(k):
         cols = pl.ds(k * wide, wide)
-        own1.append([pltpu.make_async_copy(
-            out_b.at[span(ex * 48, 48), cols], br.at[span(ex * 48, 48), cols], l_s.at[k])])
-        d1.append([])
-        for h in range(2):
-            piece = pl.ds(h * half + k * fold, fold)
-            own1[k].append(pltpu.make_async_copy(
-                row_a.at[span(dp * 96, 96), piece], ar.at[span(dp * 96, 96), piece],
-                l_s.at[2 + k * 2 + h]))
-            for d, dc in DPS:
-                yy, cc = (y + d) % 4, (c + dc) % 2
-                n = (d * 2 + dc) * 2 + h
-                d1[k].append(remote(
-                    row_a.at[span((yy * 2 + cc) * 96, 96), piece],
-                    ar.at[span(dp * 96, 96), piece], d1_s.at[k, n], d1_r.at[k, n], yy, cc, x, z))
-        c1.append([])
-        for dx, dz in PLANE:
-            xx, zz = (x + dx) % 4, (z + dz) % 4
-            n = dx * 4 + dz
-            c1[k].append(remote(
-                out_b.at[span((xx * 4 + zz) * 48, 48), cols], br.at[span(ex * 48, 48), cols],
-                c1_s.at[k, n], c1_r.at[k, n], y, c, xx, zz))
-        for cp in own1[k] + d1[k] + c1[k]:
+        return pltpu.make_async_copy(
+            out_b.at[span(ex * 48, 48), cols], br.at[span(ex * 48, 48), cols], l_s.at[k])
+
+    def own_row(k, h):
+        piece = pl.ds(h * half + k * fold, fold)
+        return pltpu.make_async_copy(
+            row_a.at[span(dp * 96, 96), piece], ar.at[span(dp * 96, 96), piece],
+            l_s.at[2 + k * 2 + h])
+
+    def compute(xv, gv, wg, wu, wd, ga, ua, hid_a, hid_b, hg, gu, in_s):
+        loads = [pltpu.make_async_copy(s, t, in_s.at[n]) for n, (s, t) in enumerate((
+            (gate_w, wg), (rows_in, xv), (up_w, wu), (down_w, wd), (grads_in, gv)))]
+        for cp in loads:
             cp.start()
-    for k in range(CHUNKS):
-        thin, cols = pl.ds(k * fold, fold), pl.ds(k * wide, wide)
-        for cp in own1[k]:
+        for cp in loads[:3]:
             cp.wait()
-        for cp in c1[k]:
-            cp.wait_recv()
-        for s in range(4):
-            band = pl.ds(s * 256, 256)
-            part[band, cols] = jnp.dot(
-                wbig_t[band, :], br[:, cols], preferred_element_type=F32).astype(BF16)
-        sb.append(remote(part.at[span((1 - c) * 512, 512), cols], sibr.at[:, cols],
-                         sb_s.at[k], sb_r.at[k], y, 1 - c, x, z))
-        sb[k].start()
-        for cp in d1[k]:
-            cp.wait_recv()
-        for q in range(4):
+
+        @pl.loop(0, 2)
+        def _(i):
+            band = pl.ds(pl.multiple_of(i * 384, 384), 384)
+            ga[band, :] = jnp.dot(xv[band, :], wg[...], preferred_element_type=F32)
+            ua[band, :] = jnp.dot(xv[band, :], wu[...], preferred_element_type=F32)
+            g = ga[band, :]
+            hid_a[band, :] = (g * jax.nn.sigmoid(g) * ua[band, :]).astype(BF16)
+
+        hid_b[...] = jnp.dot(pab[...], hid_a[...], preferred_element_type=F32).astype(BF16)
+        loads[3].wait()
+        for k in range(CHUNKS):
+            cols = pl.ds(k * wide, wide)
+            for dx in (1, 3, 2, 0):
+                band = span((x + dx) % 4 * 192, 192)
+                out_b[band, cols] = jnp.dot(
+                    hid_b[band, :], wd[:, cols], preferred_element_type=F32).astype(BF16)
+                for cp in c1_copies(k, dx):
+                    cp.start()
+            own_out(k).start()
+        loads[4].wait()
+
+        @pl.loop(0, 2)
+        def _(i):
+            band = pl.ds(pl.multiple_of(i * 384, 384), 384)
+            hg[band, :] = lax.dot_general(gv[band, :], wd[...], last, preferred_element_type=F32)
+
+        high = hg[...].astype(BF16)
+        low = (hg[...] - high.astype(F32)).astype(BF16)
+        hg[...] = (jnp.dot(pba[...], high, preferred_element_type=F32)
+                   + jnp.dot(pba[...], low, preferred_element_type=F32))
+
+        @pl.loop(0, 4)
+        def _(i):
+            band = pl.ds(pl.multiple_of(i * 192, 192), 192)
+            g, h = ga[band, :], hg[band, :]
+            sg = jax.nn.sigmoid(g)
+            gu[band, 0:384] = (h * ua[band, :] * sg * (1.0 + g * (1.0 - sg))).astype(BF16)
+            gu[band, 384:768] = (h * (g * sg)).astype(BF16)
+
+        for k in range(CHUNKS):
             for h in range(2):
                 piece = pl.ds(h * half + k * fold, fold)
-                tot[(q * 2 + h) * 96:(q * 2 + h + 1) * 96, :] = (
-                    ar[q * 96:(q + 1) * 96, piece].astype(F32)
-                    + ar[384 + q * 96:384 + (q + 1) * 96, piece].astype(F32)).astype(BF16)
-        for h in range(4):
-            band = pl.ds(h * 192, 192)
-            back[band, thin] = jnp.dot(
-                pi_t[band, :], tot[...], preferred_element_type=F32).astype(BF16)
-        d2.append([])
-        for dx, dz in PLANE:
-            xx, zz = (x + dx) % 4, (z + dz) % 4
-            n = dx * 4 + dz
-            d2[k].append(remote(
-                back.at[span((xx * 4 + zz) * 48, 48), thin], backr.at[span(ex * 48, 48), thin],
-                d2_s.at[k, n], d2_r.at[k, n], y, c, xx, zz))
-        own2.append([pltpu.make_async_copy(
-            back.at[span(ex * 48, 48), thin], backr.at[span(ex * 48, 48), thin], l_s.at[6 + k])])
-        for cp in d2[k] + own2[k]:
+
+                @pl.loop(0, 2)
+                def _(i):
+                    band = pl.ds(pl.multiple_of(i * 384, 384), 384)
+                    row_a[band, piece] = (
+                        lax.dot_general(gu[band, 0:384], wg[piece, :], last,
+                                        preferred_element_type=F32)
+                        + lax.dot_general(gu[band, 384:768], wu[piece, :], last,
+                                          preferred_element_type=F32)).astype(BF16)
+
+                for cp in d1_copies(k, h):
+                    cp.start()
+                own_row(k, h).start()
+
+        @pl.loop(0, 8)
+        def _(i):
+            cols = pl.ds(pl.multiple_of(i * 512, 512), 512)
+            wd[:, cols] = lax.dot_general(
+                hid_b[...], gv[:, cols], first, preferred_element_type=F32).astype(BF16)
+
+        @pl.loop(0, 16)
+        def _(i):
+            cols = pl.ds(pl.multiple_of(i * 256, 256), 256)
+            both = lax.dot_general(
+                xv[:, cols], gu[...], first, preferred_element_type=F32).astype(BF16)
+            wg[cols, :] = both[:, 0:384]
+            wu[cols, :] = both[:, 384:768]
+
+        saves = [pltpu.make_async_copy(s, t, in_s.at[5 + n]) for n, (s, t) in enumerate((
+            (wg, gate_g), (wu, up_g), (wd, down_g)))]
+        for cp in saves:
             cp.start()
-        sb[k].wait_recv()
-        sibr[:, cols] = (part[span(c * 512, 512), cols].astype(F32)
-                         + sibr[:, cols].astype(F32)).astype(BF16)
-        c2.append([])
-        spot = partr.at[span(y * 128, 128), cols]
-        for d in (1, 3, 2):
-            yy = (y + d) % 4
-            c2[k].append(remote(sibr.at[span(yy * 128, 128), cols], spot,
-                                c2_s.at[k, d], c2_r.at[k, d], yy, c, x, z))
-            c2[k][-1].start()
-        own2[k].append(pltpu.make_async_copy(sibr.at[span(y * 128, 128), cols], spot,
-                                             l_s.at[8 + k]))
-        own2[k][-1].start()
-    for k in range(CHUNKS):
-        thin, cols = pl.ds(k * fold, fold), pl.ds(k * wide, wide)
-        for cp in own2[k]:
+        for cp in saves:
             cp.wait()
-        for cp in c2[k] + d2[k]:
-            cp.wait_recv()
-        for h in range(2):
-            tok[:, pl.ds(h * half + k * fold, fold)] = jnp.dot(
-                placer_t[h], backr[:, thin], preferred_element_type=F32).astype(BF16)
-        moe[:, cols] = sum(
-            partr[s * 128:(s + 1) * 128, cols].astype(F32) for s in range(4)).astype(BF16)
-    for cp in sum(c1 + d1 + c2 + d2, sb):
-        cp.wait_send()
+
+    w = out_b.shape[1]
+    pl.run_scoped(
+        compute, vm(768, w), vm(768, w), vm(w, 384), vm(w, 384), vm(384, w),
+        pltpu.VMEM((768, 384), F32), pltpu.VMEM((768, 384), F32), vm(768, 384), vm(768, 384),
+        pltpu.VMEM((768, 384), F32), vm(768, 768), pltpu.SemaphoreType.DMA((8,)))
+
+    def combine(brl, arl, tot, part, sibl, summed, back, in_s):
+        c1 = [sum((c1_copies(k, dx) for dx in range(4)), []) for k in range(CHUNKS)]
+        d1 = [d1_copies(k, 0) + d1_copies(k, 1) for k in range(CHUNKS)]
+        sb, c2, d2, own2 = [], [], [], []
+        for k in range(CHUNKS):
+            thin, cols = pl.ds(k * fold, fold), pl.ds(k * wide, wide)
+            for cp in (own_out(k), own_row(k, 0), own_row(k, 1)):
+                cp.wait()
+            for cp in c1[k]:
+                cp.wait_recv()
+            load = pltpu.make_async_copy(br.at[:, cols], brl, in_s.at[0])
+            load.start()
+            load.wait()
+            for s in range(4):
+                band = pl.ds(s * 256, 256)
+                part[band, cols] = jnp.dot(
+                    wbig_t[band, :], brl[...], preferred_element_type=F32).astype(BF16)
+            sb.append(remote(part.at[span((1 - c) * 512, 512), cols], sibr.at[:, cols],
+                             sb_s.at[k], sb_r.at[k], y, 1 - c, x, z))
+            sb[k].start()
+            for cp in d1[k]:
+                cp.wait_recv()
+            more = [pltpu.make_async_copy(
+                ar.at[:, pl.ds(h * half + k * fold, fold)], arl.at[h], in_s.at[1 + h])
+                for h in range(2)]
+            for cp in more:
+                cp.start()
+            for cp in more:
+                cp.wait()
+            for q in range(4):
+                for h in range(2):
+                    tot[(q * 2 + h) * 96:(q * 2 + h + 1) * 96, :] = (
+                        arl[h, q * 96:(q + 1) * 96, :].astype(F32)
+                        + arl[h, 384 + q * 96:384 + (q + 1) * 96, :].astype(F32)).astype(BF16)
+            for h in range(4):
+                band = pl.ds(h * 192, 192)
+                back[band, thin] = jnp.dot(
+                    pi_t[band, :], tot[...], preferred_element_type=F32).astype(BF16)
+            d2.append([])
+            for dx, dz in PLANE:
+                xx, zz = (x + dx) % 4, (z + dz) % 4
+                n = dx * 4 + dz
+                d2[k].append(remote(
+                    back.at[span((xx * 4 + zz) * 48, 48), thin],
+                    backr.at[span(ex * 48, 48), thin],
+                    d2_s.at[k, n], d2_r.at[k, n], y, c, xx, zz))
+            own2.append([pltpu.make_async_copy(
+                back.at[span(ex * 48, 48), thin], backr.at[span(ex * 48, 48), thin],
+                l_s.at[6 + k])])
+            for cp in d2[k] + own2[k]:
+                cp.start()
+            sb[k].wait_recv()
+            load = pltpu.make_async_copy(sibr.at[:, cols], sibl, in_s.at[3])
+            load.start()
+            load.wait()
+            summed[:, cols] = (part[span(c * 512, 512), cols].astype(F32)
+                               + sibl[...].astype(F32)).astype(BF16)
+            c2.append([])
+            spot = partr.at[span(y * 128, 128), cols]
+            for d in (1, 3, 2):
+                yy = (y + d) % 4
+                c2[k].append(remote(summed.at[span(yy * 128, 128), cols], spot,
+                                    c2_s.at[k, d], c2_r.at[k, d], yy, c, x, z))
+                c2[k][-1].start()
+            own2[k].append(pltpu.make_async_copy(summed.at[span(y * 128, 128), cols], spot,
+                                                 l_s.at[8 + k]))
+            own2[k][-1].start()
+        for k in range(CHUNKS):
+            thin, cols = pl.ds(k * fold, fold), pl.ds(k * wide, wide)
+            for cp in own2[k]:
+                cp.wait()
+            for cp in c2[k] + d2[k]:
+                cp.wait_recv()
+            for h in range(2):
+                tok[:, pl.ds(h * half + k * fold, fold)] = jnp.dot(
+                    placer_t[h], backr[:, thin], preferred_element_type=F32).astype(BF16)
+            moe[:, cols] = sum(
+                partr[s * 128:(s + 1) * 128, cols].astype(F32) for s in range(4)).astype(BF16)
+        for cp in sum(c1 + d1 + c2 + d2, sb):
+            cp.wait_send()
+
+    pl.run_scoped(
+        combine, vm(768, wide), vm(2, 768, fold), vm(768, fold), vm(1024, w), vm(512, wide),
+        vm(512, w), vm(768, half), pltpu.SemaphoreType.DMA((4,)))
 
 
 VM = pl.BlockSpec(memory_space=pltpu.VMEM)
@@ -257,19 +383,19 @@
     )(xs, og, wts, pi, spread)
 
 
-def call_homeward(out_b, row_a, wbig_t, pi_t, placer_t):
-    w, k = out_b.shape[1], CHUNKS
+def call_experts(*args):
+    w, k = args[0].shape[1], CHUNKS
     return pl.pallas_call(
-        homeward,
-        out_shape=(out(128, w), out(128, w)),
-        in_specs=[HB, HB, VM, VM, VM],
-        out_specs=(VM, VM),
+        experts,
+        out_shape=(out(128, w), out(128, w), out(w, 384), out(w, 384), out(384, w),
+                   out(768, w), out(768, w), out(512, w)),
+        in_specs=[HB] * 5 + [VM] * 5,
+        out_specs=(VM, VM) + (HB,) * 6,
         scratch_shapes=[
-            vm(768, w), vm(768, w), vm(768, w // 2 // k), vm(1024, w), vm(512, w), vm(512, w),
-            vm(768, w // 2), vm(768, w // 2),
+            vm(768, w), vm(768, w), vm(512, w), vm(768, w // 2),
             *sems((k, 16), (k, 16), (k,), (k, 4), (k, 16)), pltpu.SemaphoreType.DMA((10,))],
-        compiler_params=pltpu.CompilerParams(has_side_effects=True, vmem_limit_bytes=58 << 20),
-    )(out_b, row_a, wbig_t, pi_t, placer_t)
+        compiler_params=pltpu.CompilerParams(has_side_effects=True, vmem_limit_bytes=60 << 20),
+    )(*args)
 
 
 def one_hot(index, size):
@@ -285,14 +411,6 @@
     before = jnp.dot(earlier, hit.astype(BF16), preferred_element_type=F32)
     rank = jnp.sum(jnp.where(hit, before, 0.0), axis=1).astype(jnp.int32)
     return rank.reshape(tok_rows, route_count)
-
-
-def to_b(a):
-    return a.reshape(8, 16, 6, -1).transpose(1, 0, 2, 3).reshape(768, -1)
-
-
-def to_a(b):
-    return b.reshape(16, 8, 6, -1).transpose(1, 0, 2, 3).reshape(768, -1)
 
 
 def on_device(tokens, expert_ids, gate_num, out_grad, gate_weight, up_weight, down_weight):
@@ -318,36 +436,14 @@
     spread = jnp.stack([
         one_hot(jnp.where(source == s % 4 * 2 + s // 4, home, -1), 96) for s in range(8)])
     rows_in, grads_in, wbig = call_dispatch(xs, out_grad, wts.astype(BF16), pi, spread)
-    gate_block, up_block, down_block = gate_weight[0], up_weight[0], down_weight[0]
-    gate_act = jnp.dot(rows_in, gate_block, preferred_element_type=F32)
-    up_act = jnp.dot(rows_in, up_block, preferred_element_type=F32)
-    sigmoid_gate = jax.nn.sigmoid(gate_act)
-    silu_gate = gate_act * sigmoid_gate
-    hidden = to_b((silu_gate * up_act).astype(BF16))
-    out_b = jnp.dot(hidden, down_block, preferred_element_type=F32).astype(BF16)
-    last = (((1,), (1,)), ((), ()))
-    first = (((0,), (0,)), ((), ()))
-    hidden_grad = to_a(lax.dot_general(grads_in, down_block, last, preferred_element_type=F32))
-    up_grad_act = (hidden_grad * silu_gate).astype(BF16)
-    gate_grad_act = (
-        hidden_grad * up_act * sigmoid_gate * (1.0 + gate_act * (1.0 - sigmoid_gate))
-    ).astype(BF16)
-    row_part = lax.dot_general(gate_grad_act, gate_block, last, preferred_element_type=F32)
-    row_part = row_part + lax.dot_general(
-        up_grad_act, up_block, last, preferred_element_type=F32
-    )
-    moe_out, token_grad = call_homeward(
-        out_b, row_part.astype(BF16), wbig.T, pi.T, jnp.stack([p.T for p in placer]))
-    down_grad = lax.dot_general(hidden, grads_in, first, preferred_element_type=F32)
-    gate_grad = lax.dot_general(rows_in, gate_grad_act, first, preferred_element_type=F32)
-    up_grad = lax.dot_general(rows_in, up_grad_act, first, preferred_element_type=F32)
-    return (
-        moe_out,
-        token_grad,
-        gate_grad.astype(BF16)[None],
-        up_grad.astype(BF16)[None],
-        down_grad.astype(BF16)[None],
-    )
+    order = j % 48 // 6 * 96 + j // 48 * 6 + j % 6
+    pab = one_hot(order, 768)
+    back = j % 96 // 6 * 48 + j // 96 * 6 + j % 6
+    pba = one_hot(back, 768)
+    moe_out, token_grad, gate_grad, up_grad, down_grad, *_ = call_experts(
+        rows_in, grads_in, gate_weight[0], up_weight[0], down_weight[0], wbig.T, pi.T,
+        jnp.stack([p.T for p in placer]), pab, pba)
+    return moe_out, token_grad, gate_grad[None], up_grad[None], down_grad[None]
 
 
 def solution(mesh):

time: 387 us -> 331 us (0.86)
  matrix products: 72 us -> 2.87 us
  Pallas kernels: 275 us -> 295 us
  local copies, waits for them, and re-layouts: 26.6 us -> 16.6 us
    dot_general x9 -> x0, matrix products: 69.2 us -> none  [the longest x1 10 us: on_device(): lax.dot_general(grads_in, down_block, last, preferred_element_type=F32)]
    pallas_call x1, Pallas kernels: 138 us -> 158 us  [call_experts(): pl.pallas_call(experts, out_shape=(out(128, w), out(128, w), out(w, 384),...]
    unnamed x31 -> x14, local copies, waits for them, and re-layouts: 2.94 us -> 13.2 us
    dot_general x1 -> x0, local copies, waits for them, and re-layouts: 10.1 us -> none  [on_device(): lax.dot_general(grads_in, down_block, last, preferred_element_type=F32)]
    reshape x3 -> x0, local copies, waits for them, and re-layouts: 6.51 us -> none  [the longest x2 4.08 us: to_b(): return a.reshape(8, 16, 6, -1).transpose(1, 0, 2, 3).reshape(768, -1)]
where the time goes in v3:
time: 331 us; the launch traced here: 326 us
  Pallas kernels  295 us (89%)
  local copies, waits for them, and re-layouts  16.6 us (5%)
  other arithmetic  10.9 us (3%)
    pallas_call x1, Pallas kernels, call_experts(): pl.pallas_call(experts, out_shape=(out(128, w), out(128, w), out(w, 384),...  158 us
    pallas_call x1, Pallas kernels, call_dispatch(): pl.pallas_call(dispatch, out_shape=(out(768, w), out(768, w), out(768, 10...  137 us
    unnamed x14, local copies, waits for them, and re-layouts  13.2 us

profile of v3, /device:TPU:1, one launch (start us, length us, event | category | flops | bytes accessed | tf_op | source)
XLA Modules:
  0.0 326.5 jit_solution(10461244127586955018)
XLA Ops:
  0.6 0.7 broadcast_compare_fusion
  1.3 0.7 convert_multiply_fusion
  2.0 0.7 broadcast_multiply_fusion
  3.0 0.1 copy.28
  3.2 0.8 copy.25
  4.1 0.2 fusion.4
  4.6 0.2 slice_reduce_fusion.1
  4.8 0.7 add_convert_fusion.4.wts
  5.8 0.1 add_convert_fusion.1
  5.9 0.8 pad_maximum_fusion.placer_t
  6.8 0.2 fusion.11
  7.0 0.2 fusion.12
  7.2 0.2 fusion.13
  7.4 0.2 fusion.14
  7.6 0.2 fusion.15
  7.8 0.2 fusion.16
  8.1 0.2 fusion.17
  8.3 0.2 fusion.18
  8.5 1.5 stack.7.spread
  10.1 1.2 fusion.3.pba
  11.3 2.7 convolution_convert_fusion.xs
  14.0 2.2 fusion.1
  16.2 136.6 %shard_map.110 = (bf16[768,4096]{1,0:T(8,128)(2,1)}, bf16[768,4096]{1,0:T(8,128)(2,1)}, bf16[768,1024]{1,0:T(8,128)(2,1)}) custom-call(bf16[768,2048]{1,0:T(8,128)(2,1)} %convolution_convert_fusion.xs, bf16[128,4096]{1,0:T(8,128)(2,1)} %og.1, bf16[384,128]{1,0:T(8,128)(2,1)} %add_convert_fusion.4.wts, bf16[768,768]{1,0:T(8,128)(2,1)} %get-tuple-element.30.pi, ...), custom_call_target="tpu_custom_call" | custom-call | tf_op jit(solution)/shard_map/pallas_call | solution.py:373
  152.8 2.6 copy.34
  155.4 158.4 %shard_map.111 = (bf16[128,4096]{1,0:T(8,128)(2,1)}, bf16[128,4096]{1,0:T(8,128)(2,1)}, bf16[4096,384]{1,0:T(8,128)(2,1)}, bf16[4096,384]{1,0:T(8,128)(2,1)}, bf...) custom-call(bf16[768,4096]{1,0:T(8,128)(2,1)} %get-tuple-element.13., ...), custom_call_target="tpu_custom_call" | custom-call | tf_op jit(solution)/shard_map/pallas_call | solution.py:388
  313.8 2.4 copy.47
  316.2 2.3 copy.48
  318.5 1.7 copy.49
  320.2 1.4 copy-done.1
  321.5 1.7 copy.50
  323.2 1.4 copy-done
  324.6 1.7 copy.51
  (29 shorter events, 1.1 us)
Async XLA Ops:
  5.5 4.5 %copy-start.3 = (bf16[128,4096]{1,0:T(8,128)(2,1)S(1)}, bf16[128,4096]{1,0:T(8,128)(2,1)}, u32[]{:S(2)}) copy-start(bf16[128,4096]{1,0:T(8,128)(2,1)} %param.7) | copy-start | bytes 3145732
  313.8 4.7 %copy-start.2 = (bf16[4096,384]{1,0:T(8,128)(2,1)S(1)}, bf16[4096,384]{1,0:T(8,128)(2,1)}, u32[]{:S(2)}) copy-start(bf16[4096,384]{1,0:T(8,128)(2,1)} %get-tuple-element.18) | copy-start | bytes 9437188
  318.5 3.0 copy-start.1
  321.5 3.0 copy-start

commit v4 on v3

--- a/solution.py
+++ b/solution.py
@@ -1,5 +1,6 @@
 import jax
 import jax.numpy as jnp
+import numpy as np
 from jax import lax
 from jax.experimental import pallas as pl
 from jax.experimental.pallas import tpu as pltpu
@@ -29,7 +30,7 @@
         device_id=(yy * 2 + cc, xx * 4 + zz), device_id_type=MESH)
 
 
-def dispatch(xs, og, wts, pi, spread, x_out, g_out, wbig, a1r, a2s, ogr, wr, b2s, a1_s, a1_r,
+def dispatch(xs, og, wts, pi, spread, x_out, g_out, wbig_t, wbig, a1r, a2s, ogr, wr, b2s, a1_s, a1_r,
              b1_s, b1_r, sb_s, sb_r, w_s, w_r, a2_s, a2_r, b2_s, b2_r, l_s):
     y, c, x, z = place()
     dp, ex = y * 2 + c, x * 4 + z
@@ -72,6 +73,8 @@
     for s in range(8):
         wbig[:, s * 128:(s + 1) * 128] = jnp.dot(
             spread[s], wr[s], preferred_element_type=F32).astype(BF16)
+        wbig_t[s * 128:(s + 1) * 128, :] = lax.dot_general(
+            wr[s], spread[s], (((0,), (1,)), ((), ())), preferred_element_type=F32).astype(BF16)
     for k in range(CHUNKS):
         thin, cols = pl.ds(k * fold, fold), pl.ds(k * wide, wide)
         for d, cp in zip((1, 3, 2), b1[k]):
@@ -118,7 +121,8 @@
             b2[k].append(remote(b2s.at[span((xx * 4 + zz) * 48, 48), cols], spot,
                                 b2_s.at[k, n], b2_r.at[k, n], y, c, xx, zz))
             b2[k][-1].start()
-        last.append(pltpu.make_async_copy(b2s.at[span(ex * 48, 48), cols], spot, l_s.at[7 + k]))
+        last.append(pltpu.make_async_copy(b2s.at[span(ex * 48, 48), cols], spot,
+                                          l_s.at[3 + 2 * CHUNKS + k]))
         last[-1].start()
     for k in range(CHUNKS):
         for cp in a2[k] + b2[k]:
@@ -173,7 +177,7 @@
         piece = pl.ds(h * half + k * fold, fold)
         return pltpu.make_async_copy(
             row_a.at[span(dp * 96, 96), piece], ar.at[span(dp * 96, 96), piece],
-            l_s.at[2 + k * 2 + h])
+            l_s.at[CHUNKS + k * 2 + h])
 
     def compute(xv, gv, wg, wu, wd, ga, ua, hid_a, hid_b, hg, gu, in_s):
         loads = [pltpu.make_async_copy(s, t, in_s.at[n]) for n, (s, t) in enumerate((
@@ -314,7 +318,7 @@
                     d2_s.at[k, n], d2_r.at[k, n], y, c, xx, zz))
             own2.append([pltpu.make_async_copy(
                 back.at[span(ex * 48, 48), thin], backr.at[span(ex * 48, 48), thin],
-                l_s.at[6 + k])])
+                l_s.at[3 * CHUNKS + k])])
             for cp in d2[k] + own2[k]:
                 cp.start()
             sb[k].wait_recv()
@@ -331,7 +335,7 @@
                                     c2_s.at[k, d], c2_r.at[k, d], yy, c, x, z))
                 c2[k][-1].start()
             own2[k].append(pltpu.make_async_copy(summed.at[span(y * 128, 128), cols], spot,
-                                                 l_s.at[8 + k]))
+                                                 l_s.at[4 * CHUNKS + k]))
             own2[k][-1].start()
         for k in range(CHUNKS):
             thin, cols = pl.ds(k * fold, fold), pl.ds(k * wide, wide)
@@ -372,13 +376,13 @@
     w, k = og.shape[1], CHUNKS
     return pl.pallas_call(
         dispatch,
-        out_shape=(out(768, w), out(768, w), out(768, 1024)),
+        out_shape=(out(768, w), out(768, w), out(1024, 768)),
         in_specs=[VM] * 5,
         out_specs=(HB, HB, VM),
         scratch_shapes=[
-            vm(768, w // 2), vm(384, w), vm(1024, w), vm(8, 96, 128), vm(768, w),
+            vm(768, 1024), vm(768, w // 2), vm(384, w), vm(1024, w), vm(8, 96, 128), vm(768, w),
             *sems((k, 16), (k, 4), (k, 4), (8,), (k, 16), (k, 16)),
-            pltpu.SemaphoreType.DMA((9,))],
+            pltpu.SemaphoreType.DMA((3 + 3 * k,))],
         compiler_params=pltpu.CompilerParams(has_side_effects=True, vmem_limit_bytes=56 << 20),
     )(xs, og, wts, pi, spread)
 
@@ -393,13 +397,23 @@
         out_specs=(VM, VM) + (HB,) * 6,
         scratch_shapes=[
             vm(768, w), vm(768, w), vm(512, w), vm(768, w // 2),
-            *sems((k, 16), (k, 16), (k,), (k, 4), (k, 16)), pltpu.SemaphoreType.DMA((10,))],
+            *sems((k, 16), (k, 16), (k,), (k, 4), (k, 16)), pltpu.SemaphoreType.DMA((5 * k,))],
         compiler_params=pltpu.CompilerParams(has_side_effects=True, vmem_limit_bytes=60 << 20),
     )(*args)
 
 
 def one_hot(index, size):
-    return (index[:, None] == jnp.arange(size, dtype=jnp.int32)[None, :]).astype(BF16)
+    return (index[:, None] == np.arange(size)[None, :]).astype(jnp.bfloat16)
+
+
+def orders():
+    j = np.arange(768)
+    pi = one_hot(j % 96 // 6 * 48 + j // 96 % 2 * 24 + j // 192 * 6 + j % 6, 768)
+    pab = one_hot(j % 48 // 6 * 96 + j // 48 * 6 + j % 6, 768)
+    home, source = j // 48 * 6 + j % 6, j % 48 // 6
+    spread = np.stack([
+        one_hot(np.where(source == s % 4 * 2 + s // 4, home, -1), 96) for s in range(8)])
+    return pi, pab, spread
 
 
 def ranks(expert_ids, expert_count):
@@ -420,29 +434,24 @@
     slot_b = expert_ids * 6 + rank
     wts = sum(jnp.where(rows == slot_b[None, :, k], gate[None, :, k], 0.0) for k in (0, 1))
     slot_a = (expert_ids % 16) * 48 + (expert_ids // 16) * 6 + rank
-    rows = jnp.arange(768, dtype=jnp.int32)[:, None]
-    placer = [
-        sum((rows == slot_a[None, :, k] + h * 24).astype(F32) for k in (0, 1)).astype(BF16)
+    rows = jnp.arange(768, dtype=jnp.int32)
+    hit = [
+        sum((rows[:, None] == slot_a[None, :, k] + h * 24).astype(F32) for k in (0, 1))
         for h in (0, 1)
     ]
+    placer = jnp.concatenate(hit, axis=1).astype(BF16)
+    placer_t = jnp.stack([
+        sum((rows[None, :] == slot_a[:, k, None] + h * 24).astype(F32) for k in (0, 1))
+        for h in (0, 1)
+    ]).astype(BF16)
     half = tokens.shape[1] // 2
     folded = jnp.concatenate([tokens[:, :half], tokens[:, half:]], axis=0)
-    xs = jnp.dot(
-        jnp.concatenate(placer, axis=1), folded, preferred_element_type=F32).astype(BF16)
-    j = jnp.arange(768, dtype=jnp.int32)
-    pi = one_hot(j % 96 // 6 * 48 + j // 96 % 2 * 24 + j // 192 * 6 + j % 6, 768)
-    home = j // 48 * 6 + j % 6
-    source = j % 48 // 6
-    spread = jnp.stack([
-        one_hot(jnp.where(source == s % 4 * 2 + s // 4, home, -1), 96) for s in range(8)])
-    rows_in, grads_in, wbig = call_dispatch(xs, out_grad, wts.astype(BF16), pi, spread)
-    order = j % 48 // 6 * 96 + j // 48 * 6 + j % 6
-    pab = one_hot(order, 768)
-    back = j % 96 // 6 * 48 + j // 96 * 6 + j % 6
-    pba = one_hot(back, 768)
+    xs = jnp.dot(placer, folded, preferred_element_type=F32).astype(BF16)
+    pi, pab, spread = orders()
+    rows_in, grads_in, wbig_t = call_dispatch(xs, out_grad, wts.astype(BF16), pi, spread)
     moe_out, token_grad, gate_grad, up_grad, down_grad, *_ = call_experts(
-        rows_in, grads_in, gate_weight[0], up_weight[0], down_weight[0], wbig.T, pi.T,
-        jnp.stack([p.T for p in placer]), pab, pba)
+        rows_in, grads_in, gate_weight[0], up_weight[0], down_weight[0], wbig_t, pi.T, placer_t,
+        pab, pab.T)
     return moe_out, token_grad, gate_grad[None], up_grad[None], down_grad[None]
 
 

time: 331 us -> 320 us (0.967)
  other arithmetic: 10.9 us -> 4.42 us
    convert_element_type x6 -> x0, other arithmetic: 3.91 us -> none  [the longest x2 3.45 us: one_hot(): (index[:, None] == jnp.arange(size, dtype=jnp.int32)[None, :]).astype(BF16)]
where the time goes in v4:
time: 320 us; the launch traced here: 317 us
  Pallas kernels  295 us (92%)
  local copies, waits for them, and re-layouts  13.9 us (4%)
  other arithmetic  4.42 us (1%)
    pallas_call x1, Pallas kernels, call_experts(): pl.pallas_call(experts, out_shape=(out(128, w), out(128, w), out(w, 384),...  158 us
    pallas_call x1, Pallas kernels, call_dispatch(): pl.pallas_call(dispatch, out_shape=(out(768, w), out(768, w), out(1024, 7...  136 us
    unnamed x14, local copies, waits for them, and re-layouts  13.2 us

profile of v4, /device:TPU:1, one launch (start us, length us, event | category | flops | bytes accessed | tf_op | source)
XLA Modules:
  0.0 317.1 jit_solution(7643165326011310578)
XLA Ops:
  0.6 0.0 copy-start.3
  0.6 0.8 broadcast_compare_fusion
  1.4 0.7 convert_multiply_fusion
  2.1 0.7 broadcast_multiply_fusion
  2.8 0.1 copy.31
  2.9 0.1 copy.36
  3.0 0.8 copy.28
  3.8 0.1 eq.188
  4.0 0.2 fusion
  4.2 0.1 convert_element_type.73
  4.3 0.1 fusion.18
  4.4 0.3 slice_reduce_fusion.1
  4.7 0.7 add_convert_fusion.4.wts
  5.4 0.1 add_convert_fusion.2
  5.5 0.1 add_convert_fusion
  5.6 0.1 add_convert_fusion.1
  5.8 0.8 pad_maximum_fusion.placer_t
  6.5 0.1 add_convert_fusion.3
  6.6 0.0 copy-done.3
  6.7 0.1 fusion.17
  6.8 2.7 convolution_convert_fusion.xs
  9.4 136.3 %shard_map.155 = (bf16[768,4096]{1,0:T(8,128)(2,1)}, bf16[768,4096]{1,0:T(8,128)(2,1)}, bf16[1024,768]{1,0:T(8,128)(2,1)}) custom-call(bf16[768,2048]{1,0:T(8,128)(2,1)} %convolution_convert_fusion.xs, bf16[128,4096]{1,0:T(8,128)(2,1)} %og.1, bf16[384,128]{1,0:T(8,128)(2,1)} %add_convert_fusion.4.wts, bf16[768,768]{1,0:T(8,128)(2,1)} %constant.50.clone.pi, ...), custom_call_target="tpu_custom_call" | custom-call | tf_op jit(solution)/shard_map/pallas_call | solution.py:377
  145.7 158.5 %shard_map.156 = (bf16[128,4096]{1,0:T(8,128)(2,1)}, bf16[128,4096]{1,0:T(8,128)(2,1)}, bf16[4096,384]{1,0:T(8,128)(2,1)}, bf16[4096,384]{1,0:T(8,128)(2,1)}, bf...) custom-call(bf16[768,4096]{1,0:T(8,128)(2,1)} %get-tuple-element.13., ...), custom_call_target="tpu_custom_call" | custom-call | tf_op jit(solution)/shard_map/pallas_call | solution.py:392
  304.2 0.0 copy-start.2
  304.2 2.4 copy.42
  306.7 2.3 copy.43
  309.0 0.0 copy-done.2
  309.0 1.7 copy.44
  310.6 1.4 copy-done.1
  312.0 1.7 copy.45
  313.6 1.4 copy-done
  315.0 1.7 copy.46
  (6 shorter events, 0.0 us)
Async XLA Ops:
  0.6 6.0 %copy-start.3 = (bf16[128,4096]{1,0:T(8,128)(2,1)S(1)}, bf16[128,4096]{1,0:T(8,128)(2,1)}, u32[]{:S(2)}) copy-start(bf16[128,4096]{1,0:T(8,128)(2,1)} %param.12) | copy-start | bytes 3145732
  304.2 4.7 %copy-start.2 = (bf16[4096,384]{1,0:T(8,128)(2,1)S(1)}, bf16[4096,384]{1,0:T(8,128)(2,1)}, u32[]{:S(2)}) copy-start(bf16[4096,384]{1,0:T(8,128)(2,1)} %get-tuple-element.18) | copy-start | bytes 9437188
  309.0 3.0 copy-start.1
  312.0 3.0 copy-start
